TPU v7x, 128 devices: a whole 4x4x4 slice. The times are simulated.
128 devices in a mesh: req: 4 (over x), exp: 32 (over z, y, core).
Axes of the slice: x: 4, y: 4, z: 4, core: 2. Of those that a mesh axis runs over, the one named last changes fastest.
Arguments:
- hidden_in: bfloat16 [4, 32, 128, 2048], P('req', 'exp'), may hold values from -6 to 6
- queries: bfloat16 [4, 32, 128, 2048], P('req', 'exp'), may hold values from -6 to 6
- suffix_pairs: bfloat16 [4, 32, 2, 128, 2048], P('req', 'exp'), may hold values from -6 to 6
- prefix_cache: bfloat16 [32, 4, 2, 384, 2048], P('exp', 'req'), may hold values from -6 to 6
- suffix_length: int32 [4, 32], P('req', 'exp'), may hold values from 1 to 128, 3072 in all within a row
- request_group: int32 [4, 32], P('req', 'exp'), may hold values from 0 to 3
- prefix_owner: int32 [32, 4], P('exp'), may hold values from 0 to 3, each once within a row
- out_weight: bfloat16 [2048, 2048], replicated, may hold values from -0.8984375 to 0.8984375
- norm_gain: float32 [2048], replicated, may hold values from 0.1 to 1.9
- routes: int32 [4, 32, 128, 8], P('req', 'exp'), may hold values from 0 to 31, all different within a row; in each aligned block of 128 rows (0 to 127, 128 to 255, ..., all dimensions but the last counted through in order) at most 40 rows name the same one
- gate_values: float32 [4, 32, 128, 8], P('req', 'exp'), may hold values from 0.05 to 0.3
- expert_upward: bfloat16 [32, 2048, 2048], P('exp'), may hold values from -0.125 to 0.125
- expert_downward: bfloat16 [32, 1024, 2048], P('exp'), may hold values from -0.1875 to 0.1875
Outputs:
- layer_out: bfloat16 [4, 32, 128, 2048], P('req', 'exp')
Inputs may be any that keep to these rules, and one draw needn't show every extreme that they name: The request at row r and column e reads the group held at prefix_cache[e, prefix_owner[e, request_group[r, e]]]. `prefix_owner`: each row is a permutation of 0 to 3. `routes`: a row names 8 different experts; on the rows of one device no expert is named more than 40 times, and on the rows of some device one expert is named exactly 40 times.
All inputs are finite; a program needn't handle non-finite values. No bound on the sum of `suffix_length` on one device may be relied on, other than what follows from the above.
Results may differ from a plain program's by a relative error of at most 0.0052.
Values may be sent and summed in bfloat16 or wider, within the bound.
A program may use at most 128 MiB of HBM per device.

v0:
```python
import jax
import jax.numpy as jnp
from jax import lax
from jax.sharding import PartitionSpec as P

HD = 128
SINK = 4


def softmax_part(scores, visible, values):
    masked = jnp.where(visible[None], scores, -jnp.inf)
    largest = jnp.max(masked, axis=2)
    weights = jnp.exp(masked - largest[:, :, None])
    totals = jnp.sum(weights, axis=2)
    summed = jnp.einsum(
        "htc,chd->htd", weights.astype(jnp.bfloat16), values, preferred_element_type=jnp.float32
    )
    return (largest, totals, summed)


def prefix_part(query_heads, cache):
    row_count = query_heads.shape[0]
    head_count = query_heads.shape[1]
    window = cache.shape[1]
    cache_keys = cache[0].reshape(window, head_count, HD)
    cache_values = cache[1].reshape(window, head_count, HD)
    scores = jnp.einsum(
        "thd,chd->htc", query_heads, cache_keys, preferred_element_type=jnp.float32
    ) * HD ** (-0.5)
    column = lax.broadcasted_iota(jnp.int32, (row_count, window), 1)
    position = lax.broadcasted_iota(jnp.int32, (row_count, window), 0)
    return softmax_part(scores, (column < SINK) | (column > position), cache_values)


def suffix_part(query_heads, pairs):
    row_count = query_heads.shape[0]
    head_count = query_heads.shape[1]
    own_keys = pairs[0].reshape(row_count, head_count, HD)
    own_values = pairs[1].reshape(row_count, head_count, HD)
    scores = jnp.einsum(
        "thd,shd->hts", query_heads, own_keys, preferred_element_type=jnp.float32
    ) * HD ** (-0.5)
    column = lax.broadcasted_iota(jnp.int32, (row_count, row_count), 1)
    position = lax.broadcasted_iota(jnp.int32, (row_count, row_count), 0)
    visible = column <= position
    return softmax_part(scores, visible, own_values)


def merge_parts(first, second):
    largest = jnp.maximum(first[0], second[0])
    scale_first = jnp.exp(first[0] - largest)
    scale_second = jnp.exp(second[0] - largest)
    totals = first[1] * scale_first + second[1] * scale_second
    summed = first[2] * scale_first[:, :, None] + second[2] * scale_second[:, :, None]
    merged = summed / totals[:, :, None]
    head_count = merged.shape[0]
    row_count = merged.shape[1]
    return jnp.transpose(merged, (1, 0, 2)).reshape(row_count, head_count * HD).astype(jnp.bfloat16)


def on_device(
    hidden_in,
    queries,
    suffix_pairs,
    prefix_cache,
    suffix_length,
    request_group,
    prefix_owner,
    out_weight,
    norm_gain,
    routes,
    gate_values,
    expert_upward,
    expert_downward,
):
    row_count = hidden_in.shape[2]
    width = hidden_in.shape[3]
    head_count = width // HD
    query_rows = queries[0, 0]
    query_heads = query_rows.reshape(row_count, head_count, HD)
    owner = prefix_owner[0, request_group[0, 0]]
    blank_stats = jnp.zeros((head_count, row_count), jnp.float32)
    blank_sums = jnp.zeros((head_count, row_count, HD), jnp.float32)
    carry = (blank_stats, blank_stats, blank_sums)
    piece = lax.all_gather(prefix_cache, "req", axis=1, tiled=True)
    start = jnp.int32(0)
    held = piece.shape[1]
    inside = (owner >= start) & (owner < start + held)
    offset = jnp.clip(owner, 0, held - 1)

    def attend_piece(ignored):
        cache = lax.dynamic_index_in_dim(piece[0], offset, 0, keepdims=False)
        return prefix_part(query_heads, cache)

    def keep_carry(ignored):
        return carry

    prefix_stats = lax.cond(inside, attend_piece, keep_carry, 0)
    suffix_stats = suffix_part(query_heads, suffix_pairs[0, 0])
    attention = merge_parts(prefix_stats, suffix_stats)
    mixed = jnp.dot(attention, out_weight, preferred_element_type=jnp.float32)
    residual = hidden_in[0, 0].astype(jnp.float32) + mixed
    scaled = residual * lax.rsqrt(jnp.mean(residual * residual, axis=1, keepdims=True) + 1e-05)
    normed = (scaled * norm_gain[None, :]).astype(jnp.bfloat16)
    flat_routes = routes[0, 0].reshape(-1)
    entry_count = flat_routes.shape[0]
    top_count = routes.shape[3]
    column_count = lax.axis_size("exp")
    local_count = expert_downward.shape[0]
    expert_count = local_count * column_count
    capacity = min(row_count, (row_count * top_count * 5 // (4 * expert_count) + 7) // 8 * 8)
    expert_ids = jnp.arange(expert_count, dtype=jnp.int32)
    chosen = (flat_routes[:, None] == expert_ids[None, :]).astype(jnp.int32)
    earlier = jnp.cumsum(chosen, axis=0) - chosen
    slot_rank = jnp.sum(earlier * chosen, axis=1)
    slot_of = flat_routes * capacity + slot_rank
    slot_count = expert_count * capacity
    source = (
        jnp.full((slot_count,), entry_count, jnp.int32)
        .at[slot_of]
        .set(jnp.arange(entry_count, dtype=jnp.int32))
    )
    filled = source < entry_count
    token_of = jnp.minimum(source, entry_count - 1) // top_count
    outgoing_rows = jnp.where(filled[:, None], normed[token_of], jnp.zeros((), jnp.bfloat16))
    outgoing_rows = outgoing_rows.reshape(column_count, local_count, capacity, width)
    joined = jnp.einsum(
        "sekd,edf->sekf",
        lax.all_to_all(outgoing_rows, "exp", split_axis=0, concat_axis=0, tiled=True),
        expert_upward,
        preferred_element_type=jnp.float32,
    )
    inner_width = joined.shape[3] // 2
    hidden_units = (jax.nn.silu(joined[..., :inner_width]) * joined[..., inner_width:]).astype(
        jnp.bfloat16
    )
    produced = jnp.einsum(
        "sekf,efd->sekd", hidden_units, expert_downward, preferred_element_type=jnp.float32
    ).astype(jnp.bfloat16)
    returned_rows = lax.all_to_all(produced, "exp", split_axis=0, concat_axis=0, tiled=True)
    per_entry = returned_rows.reshape(slot_count, width)[slot_of].reshape(
        row_count, top_count, width
    )
    weighted = jnp.sum(per_entry.astype(jnp.float32) * gate_values[0, 0][:, :, None], axis=1)
    combined = residual + weighted
    live_rows = jnp.arange(row_count, dtype=jnp.int32) < suffix_length[0, 0]
    layer_out = jnp.where(live_rows[:, None], combined, 0.0).astype(jnp.bfloat16)
    return layer_out.reshape(1, 1, row_count, width)


def solution(mesh):
    in_specs = (
        P("req", "exp", None, None),
        P("req", "exp", None, None),
        P("req", "exp", None, None, None),
        P("exp", "req", None, None, None),
        P("req", "exp"),
        P("req", "exp"),
        P("exp", None),
        P(),
        P(),
        P("req", "exp", None, None),
        P("req", "exp", None, None),
        P("exp", None, None),
        P("exp", None, None),
    )
    out_specs = P("req", "exp", None, None)
    return jax.shard_map(
        on_device, mesh=mesh, in_specs=in_specs, out_specs=out_specs, check_vma=False
    )
```

profile of v0, /device:TPU:0, one launch (start us, length us, event | category | flops | bytes accessed | tf_op | source)
XLA Modules:
  0.0 357.6 jit_solution(14926072692612265860)
XLA Ops:
  6.5 0.7 all-gather.2.cloned.1.call-update
  7.9 0.6 constant_dynamic-slice_fusion.2
  9.8 0.8 copy.51
  10.8 1.3 copy.41
  12.2 0.3 copy.67
  12.5 0.3 copy.48
  12.8 9.0 %reduce-window.6 = s32[32,8,128]{2,1,0:T(8,128)S(1)} reduce-window(s32[32,8,128]{2,1,0:T(8,128)S(1)} %fusion.40, s32[]{:T(128)} %constant.26.clone.1), window={size=1x1x128 pad=0_0x0_0x127_0}, to_apply=%region_6.7 | reduce-window | flops 4161536 | bytes 262148 | tf_op jit(solution)/shard_map/reduce-window
  21.9 0.1 copy.53
  22.5 4.3 %scatter_custom_fusion = s32[1280]{0:T(1024)S(1)} fusion(s32[1024]{0:T(1024)S(1)} %bitcast.118, s32[1024]{0:T(1024)S(1)} %iota.53, s32[]{:T(128)} %constant.59.clone.1), kind=kCustom, calls=%fused_computation.73 | custom fusion | bytes 5124 | tf_op jit(solution)/shard_map/scatter | solution.py:121
  27.0 0.4 fusion.51
  27.4 0.2 fusion.32
  27.6 102.5 %all-gather.2.cloned.1.call-done = bf16[1,4,2,384,2048]{4,3,2,0,1:T(8,128)(2,1)} async-done(((bf16[1,1,2,384,2048]{4,3,2,0,1:T(8,128)(2,1)}), bf16[1,4,2,384,2048]{4,3,2,0,1:T(8,128)(2,1)}) %all-gather.2.cloned.1.call-update) | async-done | bytes 12582928 | tf_op jit(solution)/shard_map/all_gather | solution.py:85
  130.0 24.1 %conditional.1 = (f32[16,128]{1,0:T(8,128)}, f32[16,128]{1,0:T(8,128)S(1)}, f32[16,128,128]{1,2,0:T(8,128)S(1)}) conditional(s32[]{:T(128)} %convert_element_type.60, () %tuple.13, (s32[]{:T(128)}, bf16[1,4,2,384,2048]{4,3,2,0,1:T(8,128)(2,1)}, bf16[128,16,128]{0,2,1:T(8,128)(2,1)S(1)}) %tuple.30), branch_computations={%region_0.1_spmd, %region_1.4_spmd} | conditional | flops 411398528 | bytes 45843268 | solution.py:98
  130.2 16.7 %copy.42 = bf16[1,4,2,384,2048]{3,4,2,1,0:T(8,128)(2,1)} copy(bf16[1,4,2,384,2048]{4,3,2,0,1:T(8,128)(2,1)} %get-tuple-element.28) | data formatting | bytes 25165824 | tf_op jit(solution)/shard_map
  147.5 2.2 constant_dynamic-slice_fusion.1
  149.7 1.4 fusion.2
  151.1 1.7 fusion.3
  152.8 1.4 fusion.1
  154.2 0.8 multiply_add_fusion
  155.0 0.4 fusion.31
  155.3 4.8 %multiply_reduce_fusion = (f32[128]{0:T(128)S(1)}, f32[128,2048]{1,0:T(8,128)S(1)}) fusion(bf16[128,2048]{0,1:T(8,128)(2,1)S(1)} %bitcast.112, bf16[2048,2048]{1,0:T(8,128)(2,1)} %param.22, bf16[1,1,128,2048]{3,2,1,0:T(8,128)(2,1)S(1)} %copy-done.3), kind=kOutput, calls=%fused_computation.42 | convolution fusion | flops 1074790272 | bytes 10486272 | tf_op jit(solution)/shard_map/dot_general | solution.py:101
  160.1 0.2 multiply_convert_fusion
  160.3 6.1 %gather_fusion = bf16[1280,2048]{1,0:T(8,128)(2,1)} fusion(bf16[128,2048]{1,0:T(8,128)(2,1)S(1)} %multiply_convert_fusion, s32[2048]{0:T(1024)S(1)} %pad_clamp_fusion), kind=kCustom, calls=%fused_computation | custom fusion | bytes 10490880 | tf_op jit(solution)/shard_map/gather | solution.py:125
  166.4 2.9 broadcast_select_fusion
  169.3 69.2 %all_to_all.10 = bf16[32,1,40,2048]{3,2,1,0:T(8,128)(2,1)S(1)} all-to-all(bf16[32,1,40,2048]{3,2,1,0:T(8,128)(2,1)S(1)} %broadcast_select_fusion), channel_id=1, replica_groups=mesh['req'=4,'exp'=32] {'exp'}, dimensions={0} | all-to-all | bytes 10485760 | tf_op jit(solution)/shard_map/all_to_all | solution.py:129
  238.6 13.9 %fusion.17 = f32[32,1,40,2048]{3,2,0,1:T(8,128)S(1)} fusion(bf16[1,2048,2048]{2,1,0:T(8,128)(2,1)} %param.26, bf16[32,1,40,2048]{3,2,1,0:T(8,128)(2,1)S(1)} %all_to_all.10), kind=kOutput, calls=%fused_computation.29 | convolution fusion | flops 10737418240 | bytes 24117248 | tf_op jit(solution)/shard_map/sekd,edf->sekf/dot_general | solution.py:127
  252.5 7.8 %convert_bitcast_fusion = bf16[32,1,40,2048]{3,2,1,0:T(8,128)(2,1)} fusion(bf16[1,1024,2048]{2,1,0:T(8,128)(2,1)S(1)} %copy-done.7, f32[32,1,40,2048]{3,2,0,1:T(8,128)S(1)} %fusion.17), kind=kOutput, calls=%fused_computation.27 | convolution fusion | flops 5379194880 | bytes 19922944 | tf_op jit(solution)/shard_map/sekf,efd->sekd/dot_general | solution.py:137
  260.2 5.2 %all-to-all-start.1 = ((bf16[32,1,40,2048]{3,2,1,0:T(8,128)(2,1)}), bf16[32,1,40,2048]{3,2,1,0:T(8,128)(2,1)}, u32[]{:S(2)}, u32[]{:S(2)}) async-start(bf16[32,1,40,2048]{3,2,1,0:T(8,128)(2,1)} %convert_bitcast_fusion), calls=%async_computation.1 | async-start | bytes 10485760 | tf_op jit(solution)/shard_map/all_to_all | solution.py:140
  266.3 64.9 %all-to-all-done.1 = bf16[32,1,40,2048]{3,2,1,0:T(8,128)(2,1)} async-done(((bf16[32,1,40,2048]{3,2,1,0:T(8,128)(2,1)}), bf16[32,1,40,2048]{3,2,1,0:T(8,128)(2,1)}, u32[]{:S(2)}, u32[]{:S(2)}) %all-to-all-start.1) | async-done | bytes 5242912 | tf_op jit(solution)/shard_map/all_to_all | solution.py:140
  331.1 12.1 %gather_fusion.1 = bf16[1024,2048]{1,0:T(8,128)(2,1)} fusion(bf16[1280,2048]{1,0:T(8,128)(2,1)} %bitcast.34, s32[1024]{0:T(1024)S(1)} %broadcast_clamp_fusion), kind=kCustom, calls=%fused_computation.1 | custom fusion | bytes 8392704 | tf_op jit(solution)/shard_map/gather | solution.py:141
  343.2 6.5 %fusion.12 = f32[128,2048]{1,0:T(8,128)S(1)} fusion(bf16[1024,2048]{1,0:T(8,128)(2,1)} %gather_fusion.1, f32[128,8]{1,0:T(8,128)S(1)} %copy.57), kind=kLoop, calls=%fused_computation.21 | loop fusion | flops 6029312 | bytes 5246976 | tf_op jit(solution)/shard_map/reduce_sum | solution.py:144
  349.7 1.0 fusion.35
  (43 shorter events, 1.3 us)
Async XLA Ops:
  6.5 1.4 copy-start
  6.5 5.5 %copy-start.2 = (bf16[1,1,2,128,2048]{4,3,2,1,0:T(8,128)(2,1)S(1)}, bf16[1,1,2,128,2048]{4,3,2,1,0:T(8,128)(2,1)}, u32[]{:S(2)}) copy-start(bf16[1,1,2,128,2048]{4,3,2,1,0:T(8,128)(2,1)} %param.17) | copy-start | bytes 3145732
  6.5 123.5 %all-gather.2.cloned.1.call-start = ((), (), s32[]{:S(2)}) async-start(), calls=%async_computation.2 | async-start | bytes 15728640 | tf_op jit(solution)/shard_map/all_gather | solution.py:85
  6.5 15.6 %copy-start.4 = (s32[1,1,128,8]{2,3,1,0:T(8,128)S(1)}, s32[1,1,128,8]{2,3,1,0:T(8,128)}, u32[]{:S(2)}) copy-start(s32[1,1,128,8]{2,3,1,0:T(8,128)} %param.24) | copy-start | bytes 12292
  154.2 1.2 copy-start.3
  155.3 4.8 %copy-start.5 = (f32[2048]{0:T(1024)S(1)}, f32[2048]{0:T(1024)}, u32[]{:S(2)}) copy-start(f32[2048]{0:T(1024)} %param.23) | copy-start | bytes 24580
  238.5 13.9 %copy-start.7 = (bf16[1,1024,2048]{2,1,0:T(8,128)(2,1)S(1)}, bf16[1,1024,2048]{2,1,0:T(8,128)(2,1)}, u32[]{:S(2)}) copy-start(bf16[1,1024,2048]{2,1,0:T(8,128)(2,1)} %param.27) | copy-start | bytes 12582916
  260.2 5.2 %copy-start.6 = (f32[1,1,128,8]{2,3,1,0:T(8,128)S(1)}, f32[1,1,128,8]{2,3,1,0:T(8,128)}, u32[]{:S(2)}) copy-start(f32[1,1,128,8]{2,3,1,0:T(8,128)} %param.25) | copy-start | bytes 12292
  260.2 70.9 %all-to-all-start.1 = ((bf16[32,1,40,2048]{3,2,1,0:T(8,128)(2,1)}), bf16[32,1,40,2048]{3,2,1,0:T(8,128)(2,1)}, u32[]{:S(2)}, u32[]{:S(2)}) async-start(bf16[32,1,40,2048]{3,2,1,0:T(8,128)(2,1)} %convert_bitcast_fusion), calls=%async_computation.1 | async-start | bytes 10485760 | tf_op jit(solution)/shard_map/all_to_all | solution.py:140
  331.1 19.6 %copy-start.1 = (s32[1,4]{1,0:T(1,128)S(1)}, s32[1,4]{1,0:T(1,128)}, u32[]{:S(2)}) copy-start(s32[1,4]{1,0:T(1,128)} %param.21) | copy-start | bytes 52
Sparse Core Ops, SparseCore 0:
  9.0 121.0 all-gather.1
where the time goes:
time: 359 us; the launch traced here: 358 us
  waiting for transfers between devices  168 us (47%)
  blocking collectives  69.2 us (19%)
  local copies, waits for them, and re-layouts  45.7 us (13%)
  matrix products  30.3 us (8%)
  other arithmetic  22.3 us (6%)
  between operations  16.2 us (5%)
  starting transfers between devices  5.22 us (1%)
    all_gather x1, waiting for transfers between devices, on_device(): piece = lax.all_gather(prefix_cache, 'req', axis=1, tiled=True)  102 us
    all_to_all x1, blocking collectives, on_device(): lax.all_to_all(outgoing_rows, 'exp', split_axis=0, concat_axis=0, tiled=T...  69.2 us
    all_to_all x1, waiting for transfers between devices, on_device(): lax.all_to_all(produced, 'exp', split_axis=0, concat_axis=0, tiled=True)  64.9 us
    another operation x3, local copies, waits for them, and re-layouts  16.8 us
    dot_general x1, matrix products, on_device(): jnp.einsum('sekd,edf->sekf', lax.all_to_all(outgoing_rows, 'exp', split_a...  13.9 us
    gather x1, local copies, waits for them, and re-layouts, on_device(): returned_rows.reshape(slot_count, width)[slot_of]  12.1 us
    another operation x3, other arithmetic  9.14 us
    dot_general x1, matrix products, on_device(): jnp.einsum('sekf,efd->sekd', hidden_units, expert_downward, preferred_ele...  7.78 us
  transfers between devices with their start and end apart: 2, of which 2 were waited for; matrix products, arithmetic and copies ran while one was open for 5% of the time, Pallas kernels for 0%

commit v1 on v0

v1 whole, which is shorter than its diff:
```python
import functools

import jax
import jax.numpy as jnp
from jax import lax
from jax.experimental import pallas as pl
from jax.experimental.pallas import tpu as pltpu
from jax.sharding import PartitionSpec as P

HD = 128
SINK = 4
SIDE = 4
CAP = 40
NEG = -1e30
MESH = pl.DeviceIdType.MESH
VMEM_LIMIT = 63 * 1024 * 1024
F32 = jnp.float32
BF16 = jnp.bfloat16
ANY = pl.BlockSpec(memory_space=pl.ANY)
VMEM = pl.BlockSpec(memory_space=pltpu.VMEM)
SMEM = pl.BlockSpec(memory_space=pltpu.SMEM)


def dot_t(a, b):
    return lax.dot_general(a, b, (((1,), (1,)), ((), ())), preferred_element_type=F32)


def dot(a, b):
    return jnp.dot(a, b, preferred_element_type=F32)


def dot_0(a, b):
    return lax.dot_general(a, b, (((0,), (0,)), ((), ())), preferred_element_type=F32)


class Copies:
    def __init__(self, send, recv):
        self.send, self.recv, self.made = send, recv, {}

    def start(self, key, src, dst, device):
        index = len(self.made)
        copy = pltpu.make_async_remote_copy(
            src_ref=src,
            dst_ref=dst,
            send_sem=self.send.at[index],
            recv_sem=self.recv.at[index],
            device_id=device,
            device_id_type=MESH,
        )
        copy.start()
        self.made[key] = copy

    def arrived(self, key):
        self.made[key].wait_recv()

    def drain(self):
        for copy in self.made.values():
            copy.wait_send()


def meet(devices):
    barrier = pltpu.get_barrier_semaphore()
    for device in devices:
        pl.semaphore_signal(barrier, inc=1, device_id=device, device_id_type=MESH)
    pl.semaphore_wait(barrier, len(devices))


def torus(req, e):
    core = lax.rem(e, 2)
    y = lax.rem(e // 2, SIDE)
    z = e // (2 * SIDE)

    def at(dz, dy):
        return (req, (lax.rem(z + dz, SIDE) * SIDE + lax.rem(y + dy, SIDE)) * 2 + core)

    return at(1, 0), at(3, 0), at(0, 1), at(0, 3)


def attend_kernel(
    flag_ref, q_ref, pairs_ref, cache_ref, weight_ref, hidden_ref, gain_ref, up_ref, down_ref, meta_ref,
    residual_ref, normed_ref, up_other, down_other, meta,
    qbuf, flags, cache, weight, part, stat, stat_t, stat_in, own_out, own_stat, relay, back, attn,
    send, recv, local,
):
    x, e = lax.axis_index("req"), lax.axis_index("exp")
    right, left, across = (
        (lax.rem(x + 1, SIDE), e),
        (lax.rem(x + 3, SIDE), e),
        (lax.rem(x + 2, SIDE), e),
    )
    other = (x, e + 1 - 2 * lax.rem(e, 2))
    rows, width = q_ref.shape
    heads = width // HD
    window = cache_ref.shape[1]
    half = rows // 2
    low, high = pl.ds(0, half), pl.ds(half, half)
    copies = Copies(send, recv)

    load_cache = pltpu.make_async_copy(cache_ref, cache, local.at[0])
    load_weight = pltpu.make_async_copy(weight_ref, weight, local.at[1])
    load_cache.start()
    load_weight.start()
    zp, zm, yp, ym = torus(x, e)
    meet([right, left, across, other, zp, zm, yp, ym])

    copies.start("q3", q_ref, qbuf.at[2], right)
    copies.start("q1", q_ref, qbuf.at[0], left)
    copies.start("f3", flag_ref, flags.at[2], right)
    copies.start("f1", flag_ref, flags.at[0], left)
    copies.start("f2", flag_ref, flags.at[1], across)
    copies.start("up", up_ref, up_other, other)
    copies.start("down", down_ref, down_other, other)

    def tell(source, tz, ty, device):
        copies.start(("m", tz, ty), source, meta.at[tz * SIDE + ty], device)

    def told(tz, ty):
        copies.arrived(("m", tz, ty))
        return meta.at[tz * SIDE + ty]

    tell(meta_ref, 3, 0, zp)
    tell(meta_ref, 1, 0, zm)
    tell(meta_ref, 0, 3, yp)
    tell(meta_ref, 0, 1, ym)
    meta[0] = meta_ref[...]

    scale = HD ** (-0.5)
    lane = lax.broadcasted_iota(jnp.int32, (rows, HD), 1)
    stat[...] = jnp.zeros_like(stat)
    own_stat[...] = jnp.zeros_like(own_stat)

    def softmax(scores, visible, values):
        masked = jnp.where(visible, scores, NEG)
        largest = jnp.max(masked, axis=1, keepdims=True)
        weights = jnp.exp(masked - largest)
        totals = jnp.sum(weights, axis=1, keepdims=True)
        return dot(weights.astype(BF16), values) / totals, largest + jnp.log(totals)

    own_c = lax.broadcasted_iota(jnp.int32, (rows, rows), 1)
    own_t = lax.broadcasted_iota(jnp.int32, (rows, rows), 0)

    @pl.loop(0, heads)
    def _(h):
        cols = pl.ds(pl.multiple_of(h * HD, HD), HD)
        out, lse = softmax(dot_t(q_ref[:, cols], pairs_ref[0, :, cols]) * scale, own_c <= own_t, pairs_ref[1, :, cols])
        own_out[:, cols] = out
        own_stat[...] = jnp.where(lane == h, lse, own_stat[...])

    def prefix(slots):
        c = lax.broadcasted_iota(jnp.int32, (rows, window), 1)
        t = lax.broadcasted_iota(jnp.int32, (rows, window), 0)
        visible = (c < SINK) | (c > t)
        valid = {}
        for d in slots:
            flag = flag_ref if d == 0 else flags.at[d - 1]
            valid[d] = flag[pl.ds(x, 1), :]

        @pl.loop(0, heads)
        def _(h):
            cols = pl.ds(pl.multiple_of(h * HD, HD), HD)
            for d in slots:
                q = q_ref[:, cols] if d == 0 else qbuf[d - 1, :, cols]
                out, lse = softmax(dot_t(q, cache[0, :, cols]) * scale, visible, cache[1, :, cols])
                part[d, :, cols] = (out * valid[d]).astype(BF16)
                stat[d] = jnp.where(lane == h, lse * valid[d], stat[d])

        for d in slots:
            stat_t[d] = jnp.transpose(stat[d])[0:heads, :]

    for d in (3, 1):
        source = told(d, 0)
        tell(source, d, 3, yp)
        tell(source, d, 1, ym)
        if d == 3:
            tell(source, 2, 0, zp)
    load_cache.wait()
    prefix([0])
    copies.arrived("q3")
    copies.start("q2a", qbuf.at[2, low], qbuf.at[1, low], right)
    copies.arrived("q1")
    copies.start("q2b", qbuf.at[0, high], qbuf.at[1, high], left)
    source = told(2, 0)
    tell(source, 2, 3, yp)
    tell(source, 2, 1, ym)
    for d in range(SIDE):
        tell(told(d, 3), d, 2, yp)
    copies.arrived("f1")
    copies.arrived("f3")
    prefix([1, 3])
    copies.start("r_high", part.at[1, high], back.at[0, high], right)
    copies.start("l_low", part.at[3, low], back.at[1, low], left)
    copies.start("s1", stat_t.at[1], stat_in.at[0], right)
    copies.start("s3", stat_t.at[3], stat_in.at[1], left)
    copies.arrived("q2a")
    copies.arrived("q2b")
    copies.arrived("f2")
    prefix([2])
    copies.start("relay_r", part.at[2, low], relay.at[0], right)
    copies.start("relay_l", part.at[2, high], relay.at[1], left)
    copies.start("s2", stat_t.at[2], stat_in.at[2], across)
    copies.arrived("relay_r")
    part[1, low, :] = part[1, low, :] + relay[0]
    copies.start("r_low", part.at[1, low], back.at[0, low], right)
    copies.arrived("relay_l")
    part[3, high, :] = part[3, high, :] + relay[1]
    copies.start("l_high", part.at[3, high], back.at[1, high], left)
    for key in ("s1", "s2", "s3", "r_high", "l_low", "r_low", "l_high"):
        copies.arrived(key)
    total_t = stat_t[0] + stat_in[0] + stat_in[1] + stat_in[2]
    stat[0] = jnp.transpose(jnp.concatenate([total_t, jnp.zeros((HD - heads, rows), F32)], axis=0))

    @pl.loop(0, heads)
    def _(h):
        cols = pl.ds(pl.multiple_of(h * HD, HD), HD)
        first = part[0, :, cols].astype(F32) + back[0, :, cols].astype(F32) + back[1, :, cols].astype(F32)
        lse_first = jnp.sum(jnp.where(lane == h, stat[0], 0.0), axis=1, keepdims=True)
        lse_own = jnp.sum(jnp.where(lane == h, own_stat[...], 0.0), axis=1, keepdims=True)
        top = jnp.maximum(lse_first, lse_own)
        a, b = jnp.exp(lse_first - top), jnp.exp(lse_own - top)
        attn[:, cols] = ((a * first + b * own_out[:, cols]) / (a + b)).astype(BF16)

    load_weight.wait()
    tile = min(256, width)

    def project(j, squares):
        cols = pl.ds(pl.multiple_of(j * tile, tile), tile)
        res = hidden_ref[:, cols].astype(F32) + dot(attn[...], weight[:, cols])
        residual_ref[:, cols] = res
        return squares + jnp.sum(res * res, axis=1, keepdims=True)

    squares = lax.fori_loop(0, width // tile, project, jnp.zeros((rows, 1), F32))
    factor = lax.rsqrt(squares / width + 1e-05)

    @pl.loop(0, width // tile)
    def _(j):
        cols = pl.ds(pl.multiple_of(j * tile, tile), tile)
        normed_ref[:, cols] = (residual_ref[:, cols] * factor * gain_ref[:, cols]).astype(BF16)

    for d in range(SIDE):
        told(d, 1)
        told(d, 2)
    copies.arrived("up")
    copies.arrived("down")
    copies.drain()


def attend(flag, queries, pairs, cache, weight, hidden, gain, upward, downward, meta):
    rows, width = queries.shape
    heads = width // HD
    sds = jax.ShapeDtypeStruct
    dma = pltpu.SemaphoreType.DMA
    return pl.pallas_call(
        attend_kernel,
        out_shape=(
            sds((rows, width), F32),
            sds((rows, width), BF16),
            sds(upward.shape, BF16),
            sds(downward.shape, BF16),
            sds((SIDE * SIDE,) + meta.shape, F32),
        ),
        in_specs=[VMEM, VMEM, VMEM, ANY, ANY, VMEM, VMEM, ANY, ANY, VMEM],
        out_specs=(VMEM, VMEM, ANY, ANY, VMEM),
        scratch_shapes=[
            pltpu.VMEM((3, rows, width), BF16),
            pltpu.VMEM((3, 8, HD), F32),
            pltpu.VMEM(cache.shape, BF16),
            pltpu.VMEM(weight.shape, BF16),
            pltpu.VMEM((4, rows, width), BF16),
            pltpu.VMEM((4, rows, HD), F32),
            pltpu.VMEM((4, heads, rows), F32),
            pltpu.VMEM((3, heads, rows), F32),
            pltpu.VMEM((rows, width), F32),
            pltpu.VMEM((rows, HD), F32),
            pltpu.VMEM((2, rows // 2, width), BF16),
            pltpu.VMEM((2, rows, width), BF16),
            pltpu.VMEM((rows, width), BF16),
            dma((36,)),
            dma((36,)),
            dma((2,)),
        ],
        compiler_params=pltpu.CompilerParams(
            collective_id=0, has_side_effects=True, vmem_limit_bytes=VMEM_LIMIT
        ),
        name="attend",
    )(flag, queries, pairs, cache, weight, hidden, gain, upward, downward, meta)


CHUNKS = (
    ((0, 0), (0, 1), (0, 3), (1, 0)),
    ((3, 0), (2, 0), (0, 2), (1, 1)),
    ((1, 3), (3, 1), (3, 3), (1, 2)),
    ((3, 2), (2, 1), (2, 3), (2, 2)),
)


def expert_kernel(
    length_ref, x_ref, meta, residual_ref, up_ref, down_ref, up_other, down_other,
    out_ref,
    tokens, up, down, picked, pmat, gslot, hid, sums, r1, r2, level, r3, r4,
    send, recv, local,
):
    req, e = lax.axis_index("req"), lax.axis_index("exp")
    zp, zm, yp, ym = torus(req, e)
    rows, width = x_ref.shape
    inner = down_ref.shape[0]
    half, quarter = rows // 2, rows // 4
    copies = Copies(send, recv)
    loads = []
    for index, (src, dst) in enumerate(
        ((up_ref, up.at[0]), (up_other, up.at[1]), (down_ref, down.at[0]), (down_other, down.at[1]))
    ):
        loads.append(pltpu.make_async_copy(src, dst, local.at[index]))
        loads[-1].start()
    meet([zp, zm, yp, ym])

    def slot(dz, dy):
        return (dz % SIDE) * SIDE + dy % SIDE

    def view(dz, dy, start, count):
        if dz % SIDE == 0 and dy % SIDE == 0:
            return x_ref.at[pl.ds(start, count)]
        return tokens.at[slot(dz, dy), pl.ds(start, count)]

    def push(kind, dz, dy, axis, step, start, count):
        device = {("z", 1): zp, ("z", -1): zm, ("y", 1): yp, ("y", -1): ym}[axis, step]
        tz, ty = (dz - step, dy) if axis == "z" else (dz, dy - step)
        key = (kind, tz % SIDE, ty % SIDE)
        copies.start(key, view(dz, dy, start, count), tokens.at[slot(tz, ty), pl.ds(start, count)], device)

    def both(kind, dz, dy, axis):
        start = half if kind == "b" else 0
        push(kind, dz, dy, axis, 1, start, half)
        push(kind, dz, dy, axis, -1, start, half)

    def pass_on(kind, dz, dy, axis):
        behind = (dz if axis == "z" else dy) == 3
        start = (half if kind == "b" else 0) + (0 if behind else quarter)
        push(kind + ("0" if behind else "1"), dz, dy, axis, 1 if behind else -1, start, quarter)

    def have(kind, dz, dy):
        far = dy == 2 if kind == "a" else dz == 2
        near_far = dz == 2 if kind == "a" else dy == 2
        split = far or (near_far and (dy == 0 if kind == "a" else dz == 0))
        if (dz, dy) == (0, 0):
            return
        for key in ([kind + "0", kind + "1"] if split else [kind]):
            if (key, dz, dy) not in waited:
                waited.add((key, dz, dy))
                copies.arrived((key, dz, dy))

    waited = set()
    both("a", 0, 0, "z")
    both("b", 0, 0, "y")
    both("a", 0, 0, "y")
    both("b", 0, 0, "z")
    for d in (3, 1):
        have("a", d, 0)
        pass_on("a", d, 0, "z")
        both("a", d, 0, "y")
        have("b", 0, d)
        pass_on("b", 0, d, "y")
        both("b", 0, d, "z")

    def pass_second(d):
        for near in (3, 1):
            have("a", d, near)
            pass_on("a", d, near, "y")
            have("b", near, d)
            pass_on("b", near, d, "z")

    ids = [e.astype(F32), (e + 1 - 2 * lax.rem(e, 2)).astype(F32)]
    span = 2 * CAP
    before = (
        lax.broadcasted_iota(jnp.int32, (rows, rows), 0) < lax.broadcasted_iota(jnp.int32, (rows, rows), 1)
    ).astype(BF16)
    slot_row = lax.broadcasted_iota(jnp.int32, (span, rows), 0).astype(F32)

    def block(dz, dy, cols):
        return x_ref[:, cols] if (dz, dy) == (0, 0) else tokens[slot(dz, dy), :, cols]

    def run_experts(chunk):
        pairs = [chunk[i:i + 2] for i in range(0, len(chunk), 2)]
        for p, pair in enumerate(pairs):
            for k in range(2):
                gates = jnp.zeros((span, 1), F32)
                for i, (dz, dy) in enumerate(pair):
                    source = slot(dz, dy)
                    named = (meta[source, 0:8, :] == ids[k]).astype(F32)
                    mine = jnp.sum(named, axis=0, keepdims=True)
                    gate = jnp.sum(named * meta[source, 8:16, :], axis=0, keepdims=True)
                    rank = dot(jnp.broadcast_to(mine, (8, rows)).astype(BF16), before)[0:1, :]
                    place = jnp.where(mine > 0.0, rank + float(i * CAP), -1.0)
                    chosen = (slot_row == place).astype(F32)
                    pmat[p, k * span:(k + 1) * span, i * rows:(i + 1) * rows] = chosen.astype(BF16)
                    gates = gates + jnp.sum(chosen * gate, axis=1, keepdims=True)
                gslot[k, p * span:(p + 1) * span, :] = jnp.broadcast_to(gates, (span, HD))
        tile = min(512, width)

        @pl.loop(0, width // tile)
        def _(j):
            cols = pl.ds(pl.multiple_of(j * tile, tile), tile)
            for p, pair in enumerate(pairs):
                joint = jnp.concatenate([block(dz, dy, cols) for dz, dy in pair], axis=0)
                rows_out = dot(pmat[p], joint).astype(BF16)
                for k in range(2):
                    picked[k, p * span:(p + 1) * span, cols] = rows_out[k * span:(k + 1) * span, :]

        count = len(pairs) * span
        tile_f = min(256, inner)

        @pl.loop(0, inner // tile_f)
        def _(j):
            start = pl.multiple_of(j * tile_f, tile_f)
            for k in range(2):
                gate = dot(picked[k, 0:count, :], up[k, :, pl.ds(start, tile_f)])
                lift = dot(picked[k, 0:count, :], up[k, :, pl.ds(pl.multiple_of(inner + start, tile_f), tile_f)])
                hid[k, 0:count, pl.ds(start, tile_f)] = (gate / (1.0 + jnp.exp(-gate)) * lift).astype(BF16)

        tile_d = min(256, width)

        @pl.loop(0, width // tile_d)
        def _(j):
            cols = pl.ds(pl.multiple_of(j * tile_d, tile_d), tile_d)
            made = []
            for k in range(2):
                gates = gslot[k, 0:count, 0:1]
                made.append((dot(hid[k, 0:count, :], down[k, :, cols]) * gates).astype(BF16))
            for p, pair in enumerate(pairs):
                joint = jnp.concatenate([m[p * span:(p + 1) * span, :] for m in made], axis=0)
                placed = dot_0(pmat[p], joint).astype(BF16)
                for i, (dz, dy) in enumerate(pair):
                    sums[slot(dz, dy), :, cols] = placed[i * rows:(i + 1) * rows, :]

    def sum_view(h, i, j, start, count):
        dz, dy = (i, j) if h == 0 else (j, i)
        return sums.at[slot(dz, dy), pl.ds(h * half + start, count)]

    first = ((yp, ym), (zp, zm))
    second = ((zp, zm), (yp, ym))

    def far_out(h, i):
        copies.start(("1+", h, i), sum_view(h, i, 2, 0, quarter), r1.at[h, i, pl.ds(0, quarter)], first[h][0])
        copies.start(("1-", h, i), sum_view(h, i, 2, quarter, quarter), r1.at[h, i, pl.ds(quarter, quarter)], first[h][1])

    def add_to(ref, other):
        ref[...] = (ref[...].astype(F32) + other[...].astype(F32)).astype(BF16)

    def near_out(h, i):
        copies.arrived(("1+", h, i))
        add_to(sum_view(h, i, 1, 0, quarter), r1.at[h, i, pl.ds(0, quarter)])
        copies.start(("2+", h, i), sum_view(h, i, 1, 0, half), r2.at[h, i, 0], first[h][0])
        copies.arrived(("1-", h, i))
        add_to(sum_view(h, i, 3, quarter, quarter), r1.at[h, i, pl.ds(quarter, quarter)])
        copies.start(("2-", h, i), sum_view(h, i, 3, 0, half), r2.at[h, i, 1], first[h][1])

    def gathered(h, i, start, count):
        copies_rows = pl.ds(start, count)
        return (
            sum_view(h, i, 0, start, count)[...].astype(F32)
            + r2[h, i, 0, copies_rows, :].astype(F32)
            + r2[h, i, 1, copies_rows, :].astype(F32)
        )

    def arrived_2(h, i):
        copies.arrived(("2+", h, i))
        copies.arrived(("2-", h, i))

    order = (2, 1, 3, 0)
    lo, hi = pl.ds(0, quarter), pl.ds(quarter, quarter)

    loads_waited = False
    for number, chunk in enumerate(CHUNKS):
        if number == 0:
            pass_second(0)
        if number == 1:
            have("a", 2, 0)
            both("a", 2, 0, "y")
            have("b", 0, 2)
            both("b", 0, 2, "z")
            pass_second(1)
        if number == 2:
            pass_second(3)
        if number == 3:
            pass_second(2)
        for dz, dy in chunk:
            have("a", dz, dy)
            have("b", dz, dy)
        if not loads_waited:
            for load in loads:
                load.wait()
            loads_waited = True
        run_experts(chunk)

    for i in order:
        for h in range(2):
            far_out(h, i)
    for i in order:
        for h in range(2):
            near_out(h, i)
    for h in range(2):
        arrived_2(h, 2)
        level[h, 2] = gathered(h, 2, 0, half).astype(BF16)
        copies.start(("3+", h), level.at[h, 2, lo], r3.at[h, lo], second[h][0])
        copies.start(("3-", h), level.at[h, 2, hi], r3.at[h, hi], second[h][1])
    for h in range(2):
        arrived_2(h, 1)
        copies.arrived(("3+", h))
        level[h, 1, lo, :] = (gathered(h, 1, 0, quarter) + r3[h, lo, :].astype(F32)).astype(BF16)
        level[h, 1, hi, :] = gathered(h, 1, quarter, quarter).astype(BF16)
        copies.start(("4+", h), level.at[h, 1], r4.at[h, 0], second[h][0])
        arrived_2(h, 3)
        copies.arrived(("3-", h))
        level[h, 3, lo, :] = gathered(h, 3, 0, quarter).astype(BF16)
        level[h, 3, hi, :] = (gathered(h, 3, quarter, quarter) + r3[h, hi, :].astype(F32)).astype(BF16)
        copies.start(("4-", h), level.at[h, 3], r4.at[h, 1], second[h][1])
    length = length_ref[0]
    for h in range(2):
        arrived_2(h, 0)
        copies.arrived(("4+", h))
        copies.arrived(("4-", h))
        span_rows = pl.ds(h * half, half)
        mixture = gathered(h, 0, 0, half) + r4[h, 0].astype(F32) + r4[h, 1].astype(F32)
        position = lax.broadcasted_iota(jnp.int32, (half, width), 0) + h * half
        out_ref[span_rows, :] = jnp.where(position < length, residual_ref[span_rows, :] + mixture, 0.0).astype(BF16)
    copies.drain()


def experts(length, normed, meta, residual, upward, downward, up_other, down_other):
    rows, width = normed.shape
    inner = downward.shape[0]
    half = rows // 2
    slots = SIDE * SIDE
    pairs = len(CHUNKS[0]) // 2
    dma = pltpu.SemaphoreType.DMA
    return pl.pallas_call(
        expert_kernel,
        out_shape=jax.ShapeDtypeStruct((rows, width), BF16),
        in_specs=[SMEM, VMEM, VMEM, VMEM, ANY, ANY, ANY, ANY],
        out_specs=VMEM,
        scratch_shapes=[
            pltpu.VMEM((slots, rows, width), BF16),
            pltpu.VMEM((2,) + upward.shape, BF16),
            pltpu.VMEM((2,) + downward.shape, BF16),
            pltpu.VMEM((2, pairs * 2 * CAP, width), BF16),
            pltpu.VMEM((pairs, 4 * CAP, 2 * rows), BF16),
            pltpu.VMEM((2, pairs * 2 * CAP, HD), F32),
            pltpu.VMEM((2, pairs * 2 * CAP, inner), BF16),
            pltpu.VMEM((slots, rows, width), BF16),
            pltpu.VMEM((2, SIDE, half, width), BF16),
            pltpu.VMEM((2, SIDE, 2, half, width), BF16),
            pltpu.VMEM((2, SIDE, half, width), BF16),
            pltpu.VMEM((2, half, width), BF16),
            pltpu.VMEM((2, 2, half, width), BF16),
            dma((112,)),
            dma((112,)),
            dma((4,)),
        ],
        compiler_params=pltpu.CompilerParams(
            collective_id=1, has_side_effects=True, vmem_limit_bytes=VMEM_LIMIT
        ),
        name="experts",
    )(length, normed, meta, residual, upward, downward, up_other, down_other)


def on_device(
    hidden_in, queries, suffix_pairs, prefix_cache, suffix_length, request_group, prefix_owner,
    out_weight, norm_gain, routes, gate_values, expert_upward, expert_downward,
):
    rows, width = hidden_in.shape[2:]
    length = suffix_length[0, 0]
    owner = prefix_owner[0, request_group[0, 0]]
    flag = (lax.broadcasted_iota(jnp.int32, (8, HD), 0) == owner).astype(F32)
    live = lax.broadcasted_iota(jnp.int32, (8, rows), 1) < length
    names = jnp.where(live, jnp.transpose(routes[0, 0]), -1).astype(F32)
    meta = jnp.concatenate([names, jnp.transpose(gate_values[0, 0])], axis=0)
    residual, normed, up_other, down_other, everyone = attend(
        flag, queries[0, 0], suffix_pairs[0, 0], prefix_cache[0, 0], out_weight, hidden_in[0, 0],
        norm_gain.reshape(1, width), expert_upward[0], expert_downward[0], meta,
    )
    out = experts(
        length.reshape(1), normed, everyone, residual, expert_upward[0], expert_downward[0], up_other, down_other
    )
    return out.reshape(1, 1, rows, width)


def solution(mesh):
    in_specs = (
        P("req", "exp", None, None),
        P("req", "exp", None, None),
        P("req", "exp", None, None, None),
        P("exp", "req", None, None, None),
        P("req", "exp"),
        P("req", "exp"),
        P("exp", None),
        P(),
        P(),
        P("req", "exp", None, None),
        P("req", "exp", None, None),
        P("exp", None, None),
        P("exp", None, None),
    )
    out_specs = P("req", "exp", None, None)
    return jax.shard_map(
        on_device, mesh=mesh, in_specs=in_specs, out_specs=out_specs, check_vma=False
    )
```

time: 359 us -> 182 us (0.51)
  Pallas kernels: 0 us -> 175 us
  waiting for transfers between devices: 168 us -> 0 us
  blocking collectives: 69.2 us -> 0 us
  local copies, waits for them, and re-layouts: 45.7 us -> 3.13 us
  matrix products: 30.3 us -> 0 us
  other arithmetic: 22.3 us -> 2.63 us
  between operations: 16.2 us -> 1.36 us
  starting transfers between devices: 5.22 us -> 0 us
    pallas_call x0 -> x2, Pallas kernels: none -> 175 us  [the longest x1 112 us: experts(): pl.pallas_call(expert_kernel, out_shape=jax.ShapeDtypeStruct((rows, width...]
    all_gather x1 -> x0, waiting for transfers between devices: 102 us -> none  [on_device(): piece = lax.all_gather(prefix_cache, 'req', axis=1, tiled=True)]
    all_to_all x1 -> x0, blocking collectives: 69.2 us -> none  [on_device(): lax.all_to_all(outgoing_rows, 'exp', split_axis=0, concat_axis=0, tiled=T...]
    all_to_all x1 -> x0, waiting for transfers between devices: 64.9 us -> none  [on_device(): lax.all_to_all(produced, 'exp', split_axis=0, concat_axis=0, tiled=True)]
    dot_general x6 -> x0, matrix products: 28.6 us -> none  [the longest x1 13.9 us: on_device(): jnp.einsum('sekd,edf->sekf', lax.all_to_all(outgoing_rows, 'exp', split_a...]
    gather x2 -> x0, local copies, waits for them, and re-layouts: 18.2 us -> none  [the longest x1 12.1 us: on_device(): returned_rows.reshape(slot_count, width)[slot_of]]
    another operation x3 -> x0, local copies, waits for them, and re-layouts: 16.8 us -> none
    another operation x3 -> x0, other arithmetic: 9.14 us -> none
  transfers between devices with their start and end apart: 2 -> 0, of which waited for: 2 -> 0; matrix products, arithmetic and copies ran while one was open for 5% -> 0% of each run, Pallas kernels for 0% -> 0%
where the time goes in v1:
time: 182 us
  Pallas kernels  175 us (96%)
  local copies, waits for them, and re-layouts  3.13 us (2%)
  other arithmetic  2.63 us (1%)
    pallas_call x1, Pallas kernels, experts(): pl.pallas_call(expert_kernel, out_shape=jax.ShapeDtypeStruct((rows, width...  112 us
    pallas_call x1, Pallas kernels, attend(): pl.pallas_call(attend_kernel, out_shape=(sds((rows, width), F32), sds((ro...  62.4 us

profile of v1, /device:TPU:0, one launch (start us, length us, event | category | flops | bytes accessed | tf_op | source)
XLA Modules:
  0.0 181.8 jit_solution(17766235436629300588)
XLA Ops:
  0.0 0.0 copy-start
  1.3 0.0 copy-done
  1.3 0.6 constant_dynamic-slice_fusion
  1.9 0.6 compare_convert_fusion
  2.6 0.7 fusion.1
  3.3 0.7 iota.13.flag_ref
  3.9 1.3 pad_maximum_fusion.meta_ref
  5.2 62.4 %attend.1 = (f32[128,2048]{1,0:T(8,128)}, bf16[128,2048]{1,0:T(8,128)(2,1)}, bf16[2048,2048]{1,0:T(8,128)(2,1)}, bf16[1024,2048]{1,0:T(8,128)(2,1)}, f32[16,16,128]{2,1,0:T(8,128)}) custom-call(f32[8,128]{1,0:T(8,128)} %iota.13.flag_ref, bf16[128,2048]{1,0:T(8,128)(2,1)} %bitcast.35, bf16[2,128,2048]{2,1,0:T(8,128)(2,1)} %bitcast.34, ...), custom_call_target="tpu_custom_call" | custom-call | tf_op jit(solution)/shard_map/attend/pallas_call | solution.py:252
  67.6 112.4 %experts.1 = bf16[128,2048]{1,0:T(8,128)(2,1)} custom-call(s32[1]{0:T(128)} %bitcast.23.length_ref, bf16[128,2048]{1,0:T(8,128)(2,1)} %get-tuple-element.10.x_ref, f32[16,16,128]{2,1,0:T(8,128)} %get-tuple-element.11.meta, f32[128,2048]{1,0:T(8,128)} %get-tuple-element.12.residual_ref, bf16[2048,2048]{1,0:T(8,128)(2,1)} %bitcast.29, ...), custom_call_target="tpu_custom_call" | custom-call | tf_op jit(solution)/shard_map/experts/pallas_call | solution.py:535
  180.0 1.9 %copy.17 = bf16[1,1,128,2048]{3,2,1,0:T(8,128)(2,1)} copy(bf16[1,1,128,2048]{3,2,1,0:T(8,128)(2,1)} %bitcast.33) | data formatting | bytes 1048576
  (1 shorter events, 0.0 us)
Async XLA Ops:
  0.0 1.3 copy-start

commit v2 on v1

v2 whole, which is shorter than its diff:
```python
import functools

import jax
import jax.numpy as jnp
from jax import lax
from jax.experimental import pallas as pl
from jax.experimental.pallas import tpu as pltpu
from jax.sharding import PartitionSpec as P

HD = 128
SINK = 4
SIDE = 4
CAP = 40
NEG = -1e30
MESH = pl.DeviceIdType.MESH
VMEM_LIMIT = 63 * 1024 * 1024
F32 = jnp.float32
BF16 = jnp.bfloat16
ANY = pl.BlockSpec(memory_space=pl.ANY)
VMEM = pl.BlockSpec(memory_space=pltpu.VMEM)
SMEM = pl.BlockSpec(memory_space=pltpu.SMEM)


def dot_t(a, b):
    return lax.dot_general(a, b, (((1,), (1,)), ((), ())), preferred_element_type=F32)


def dot(a, b):
    return jnp.dot(a, b, preferred_element_type=F32)


def dot_0(a, b):
    return lax.dot_general(a, b, (((0,), (0,)), ((), ())), preferred_element_type=F32)


class Copies:
    def __init__(self, send, recv):
        self.send, self.recv, self.made, self.gone = send, recv, {}, set()

    def start(self, key, src, dst, device):
        index = len(self.made)
        copy = pltpu.make_async_remote_copy(
            src_ref=src,
            dst_ref=dst,
            send_sem=self.send.at[index],
            recv_sem=self.recv.at[index],
            device_id=device,
            device_id_type=MESH,
        )
        copy.start()
        self.made[key] = copy

    def arrived(self, key):
        self.made[key].wait_recv()

    def left(self, key):
        self.made[key].wait_send()
        self.gone.add(key)

    def drain(self):
        for key, copy in self.made.items():
            if key not in self.gone:
                copy.wait_send()


def meet(devices):
    barrier = pltpu.get_barrier_semaphore()
    for device in devices:
        pl.semaphore_signal(barrier, inc=1, device_id=device, device_id_type=MESH)
    pl.semaphore_wait(barrier, len(devices))


def torus(req, e):
    core = lax.rem(e, 2)
    y = lax.rem(e // 2, SIDE)
    z = e // (2 * SIDE)

    def at(dz, dy):
        return (req, (lax.rem(z + dz, SIDE) * SIDE + lax.rem(y + dy, SIDE)) * 2 + core)

    return at(1, 0), at(3, 0), at(0, 1), at(0, 3)


GROUPS = 2
CHUNKS = (
    ((0, 0), (0, 1), (0, 3), (1, 0)),
    ((3, 0), (2, 0), (0, 2), (1, 1)),
    ((1, 3), (3, 1), (1, 2), (2, 1)),
    ((3, 3), (3, 2), (2, 3), (2, 2)),
)


def slot(dz, dy):
    return (dz % SIDE) * SIDE + dy % SIDE


def layer_kernel(
    length_ref, group_ref, owner_ref, q_ref, pairs_ref, cache_ref, weight_ref, hidden_ref, gain_ref,
    routes_ref, gates_ref, up_ref, down_ref,
    out_ref,
    qrows, flag, flags, cache, part, stat, stat_t, stat_in, own, own_stat, relay, back, attn,
    meta, tokens, up, down, pmat, gslot, hid, sums, r1, r2, r3, r4,
    send, recv, local,
):
    x, e = lax.axis_index("req"), lax.axis_index("exp")
    right, left, across = (
        (lax.rem(x + 1, SIDE), e),
        (lax.rem(x + 3, SIDE), e),
        (lax.rem(x + 2, SIDE), e),
    )
    other = (x, e + 1 - 2 * lax.rem(e, 2))
    zp, zm, yp, ym = torus(x, e)
    rows, width = q_ref.shape
    heads = width // HD
    window = cache_ref.shape[1]
    inner = down_ref.shape[0]
    half, quarter = rows // 2, rows // 4
    size = rows // GROUPS
    part_half = size // 2
    copies = Copies(send, recv)

    loads = {}
    for index, (key, src, dst) in enumerate(
        (
            ("cache", cache_ref, cache),
            ("weight", weight_ref, sums),
            ("up", up_ref, up.at[0]),
            ("down", down_ref, down.at[0]),
        )
    ):
        loads[key] = pltpu.make_async_copy(src, dst, local.at[index])
        loads[key].start()

    length = length_ref[0, 0]
    group = group_ref[0, 0]
    owner = jnp.int32(0)
    for k in range(SIDE):
        owner = jnp.where(group == k, owner_ref[0, k], owner)
    flag[...] = (lax.broadcasted_iota(jnp.int32, (8, HD), 0) == owner).astype(F32)
    live = lax.broadcasted_iota(jnp.int32, (8, rows), 1) < length
    meta[0, 0:8, :] = jnp.where(live, jnp.transpose(routes_ref[...].astype(F32)), -1.0)
    meta[0, 8:16, :] = jnp.transpose(gates_ref[...])
    meet([right, left, across, other, zp, zm, yp, ym])

    def rows_of(g, start=0, count=None):
        return pl.ds(g * size + start, size if count is None else count)

    def q_slot(d, span):
        return qrows.at[pl.ds((d - 1) * rows + span.start, span.size)]

    def q_out(g):
        copies.start(("q", 3, g), q_ref.at[rows_of(g)], q_slot(3, rows_of(g)), right)
        copies.start(("q", 1, g), q_ref.at[rows_of(g)], q_slot(1, rows_of(g)), left)

    def q_on(g):
        low, high = rows_of(g, 0, part_half), rows_of(g, part_half, part_half)
        copies.arrived(("q", 3, g))
        copies.start(("q2+", g), q_slot(3, low), q_slot(2, low), right)
        copies.arrived(("q", 1, g))
        copies.start(("q2-", g), q_slot(1, high), q_slot(2, high), left)

    q_out(0)
    copies.start("f3", flag, flags.at[2], right)
    copies.start("f1", flag, flags.at[0], left)
    copies.start("f2", flag, flags.at[1], across)

    def tell(tz, ty, source, device):
        copies.start(("m", tz, ty), meta.at[source], meta.at[slot(tz, ty)], device)

    def told(tz, ty):
        copies.arrived(("m", tz, ty))
        return slot(tz, ty)

    tell(3, 0, 0, zp)
    tell(1, 0, 0, zm)
    tell(0, 3, 0, yp)
    tell(0, 1, 0, ym)
    copies.start("up", up_ref, up.at[1], other)
    copies.start("down", down_ref, down.at[1], other)

    scale = HD ** (-0.5)
    lane = lax.broadcasted_iota(jnp.int32, (rows, HD), 1)
    lane_g = lax.broadcasted_iota(jnp.int32, (size, HD), 1)
    stat[...] = jnp.zeros_like(stat)
    own_stat[...] = jnp.zeros_like(own_stat)

    def softmax(scores, visible, values):
        masked = jnp.where(visible, scores, NEG)
        largest = jnp.max(masked, axis=1, keepdims=True)
        weights = jnp.exp(masked - largest)
        totals = jnp.sum(weights, axis=1, keepdims=True)
        return dot(weights.astype(BF16), values) * (1.0 / totals), largest + jnp.log(totals)

    def columns(h):
        return pl.ds(pl.multiple_of(h * HD, HD), HD)

    own_c = lax.broadcasted_iota(jnp.int32, (rows, rows), 1)
    own_t = lax.broadcasted_iota(jnp.int32, (rows, rows), 0)
    several = min(2, heads)

    @pl.loop(0, heads // several)
    def _(block):
        stats = own_stat[...]
        for k in range(several):
            h = block * several + k
            cols = columns(h)
            scores = dot_t(q_ref[:, cols], pairs_ref[0, :, cols]) * scale
            out, lse = softmax(scores, own_c <= own_t, pairs_ref[1, :, cols])
            own[:, cols] = out
            stats = jnp.where(lane == h, lse, stats)
        own_stat[...] = stats

    def prefix(g, slots):
        c = lax.broadcasted_iota(jnp.int32, (size, window), 1)
        t = lax.broadcasted_iota(jnp.int32, (size, window), 0) + g * size
        visible = (c < SINK) | (c > t)
        span = rows_of(g)
        valid = {d: (flag if d == 0 else flags.at[d - 1])[pl.ds(x, 1), :] for d in slots}
        several = min(4 // len(slots), heads)

        @pl.loop(0, heads // several)
        def _(block):
            stats = {d: stat[g, d, 0:size, :] for d in slots}
            for k in range(several):
                h = block * several + k
                cols = columns(h)
                for d in slots:
                    q = q_ref[span, cols] if d == 0 else q_slot(d, span)[:, cols]
                    out, lse = softmax(dot_t(q, cache[0, :, cols]) * scale, visible, cache[1, :, cols])
                    part[d, span, cols] = (out * valid[d]).astype(BF16)
                    stats[d] = jnp.where(lane_g == h, lse * valid[d], stats[d])
            for d in slots:
                stat[g, d, 0:size, :] = stats[d]

        for d in slots:
            stat_t[g, d] = jnp.transpose(stat[g, d])[0:heads, :]

    def direct_out(g):
        low, high = rows_of(g, 0, part_half), rows_of(g, part_half, part_half)
        copies.start(("r_high", g), part.at[1, high], back.at[0, high], right)
        copies.start(("l_low", g), part.at[3, low], back.at[1, low], left)
        copies.start(("s1", g), stat_t.at[g, 1], stat_in.at[g, 0], right)
        copies.start(("s3", g), stat_t.at[g, 3], stat_in.at[g, 1], left)

    def relay_out(g):
        low, high = rows_of(g, 0, part_half), rows_of(g, part_half, part_half)
        copies.start(("relay_r", g), part.at[2, low], relay.at[g, 0], right)
        copies.start(("relay_l", g), part.at[2, high], relay.at[g, 1], left)
        copies.start(("s2", g), stat_t.at[g, 2], stat_in.at[g, 2], across)

    def relay_on(g):
        low, high = rows_of(g, 0, part_half), rows_of(g, part_half, part_half)
        copies.arrived(("relay_r", g))
        part[1, low, :] = part[1, low, :] + relay[g, 0]
        copies.start(("r_low", g), part.at[1, low], back.at[0, low], right)
        copies.arrived(("relay_l", g))
        part[3, high, :] = part[3, high, :] + relay[g, 1]
        copies.start(("l_high", g), part.at[3, high], back.at[1, high], left)

    tile = min(256, width)

    def finish(g):
        for key in ("s1", "s2", "s3", "r_high", "l_low", "r_low", "l_high"):
            copies.arrived((key, g))
        span = rows_of(g)
        total_t = stat_t[g, 0] + stat_in[g, 0] + stat_in[g, 1] + stat_in[g, 2]
        stat[g, 0] = jnp.transpose(jnp.concatenate([total_t, jnp.zeros((HD - heads, rows), F32)], axis=0))
        several = min(4, heads)

        @pl.loop(0, heads // several)
        def _(block):
            for k in range(several):
                h = block * several + k
                cols = columns(h)
                first = part[0, span, cols].astype(F32) + back[0, span, cols].astype(F32) + back[1, span, cols].astype(F32)
                lse_first = jnp.sum(jnp.where(lane_g == h, stat[g, 0, 0:size, :], 0.0), axis=1, keepdims=True)
                lse_own = jnp.sum(jnp.where(lane_g == h, own_stat[span, :], 0.0), axis=1, keepdims=True)
                top = jnp.maximum(lse_first, lse_own)
                a, b = jnp.exp(lse_first - top), jnp.exp(lse_own - top)
                attn[:, cols] = ((a * first + b * own[span, cols]) * (1.0 / (a + b))).astype(BF16)

        if g == 0:
            loads["weight"].wait()

        def project(j, squares):
            cols = pl.ds(pl.multiple_of(j * tile, tile), tile)
            weight = sums[:, :, cols].reshape(width, tile)
            res = hidden_ref[span, cols].astype(F32) + dot(attn[...], weight)
            own[span, cols] = res
            return squares + jnp.sum(res * res, axis=1, keepdims=True)

        squares = lax.fori_loop(0, width // tile, project, jnp.zeros((size, 1), F32))
        factor = lax.rsqrt(squares / width + 1e-05)

        @pl.loop(0, width // tile)
        def _(j):
            cols = pl.ds(pl.multiple_of(j * tile, tile), tile)
            tokens[0, span, cols] = (own[span, cols] * factor * gain_ref[:, cols]).astype(BF16)

    def view(dz, dy, start, count):
        return tokens.at[slot(dz, dy), pl.ds(start, count)]

    def start_of(kind):
        return kind[1] * size + (part_half if kind[0] == "b" else 0)

    def push(key, dz, dy, axis, step, start, count):
        device = {("z", 1): zp, ("z", -1): zm, ("y", 1): yp, ("y", -1): ym}[axis, step]
        tz, ty = ((dz - step) % SIDE, dy) if axis == "z" else (dz, (dy - step) % SIDE)
        copies.start((key, tz, ty), view(dz, dy, start, count), view(tz, ty, start, count), device)

    def both(kind, dz, dy, axis):
        push(kind, dz, dy, axis, 1, start_of(kind), part_half)
        push(kind, dz, dy, axis, -1, start_of(kind), part_half)

    def pass_on(kind, dz, dy, axis):
        behind = (dz if axis == "z" else dy) == 3
        start = start_of(kind) + (0 if behind else part_half // 2)
        push((kind, behind), dz, dy, axis, 1 if behind else -1, start, part_half // 2)

    waited = set()

    def have(kind, dz, dy):
        first, last = (dz, dy) if kind[0] == "a" else (dy, dz)
        if first == 0 and last == 0:
            return
        split = last == 2 or (last == 0 and first == 2)
        for key in ([(kind, True), (kind, False)] if split else [kind]):
            if (key, dz, dy) not in waited:
                waited.add((key, dz, dy))
                copies.arrived((key, dz, dy))

    def spread_0(g):
        both(("a", g), 0, 0, "z")
        both(("b", g), 0, 0, "y")
        both(("a", g), 0, 0, "y")
        both(("b", g), 0, 0, "z")

    def spread_1(g):
        for d in (3, 1):
            have(("a", g), d, 0)
            pass_on(("a", g), d, 0, "z")
            both(("a", g), d, 0, "y")
            have(("b", g), 0, d)
            pass_on(("b", g), 0, d, "y")
            both(("b", g), 0, d, "z")

    def spread_far(g):
        have(("a", g), 2, 0)
        both(("a", g), 2, 0, "y")
        have(("b", g), 0, 2)
        both(("b", g), 0, 2, "z")

    def pass_second(g, d):
        for near in (3, 1):
            have(("a", g), d, near)
            pass_on(("a", g), d, near, "y")
            have(("b", g), near, d)
            pass_on(("b", g), near, d, "z")

    ids = [e.astype(F32), (e + 1 - 2 * lax.rem(e, 2)).astype(F32)]
    span2 = 2 * CAP
    count = len(CHUNKS[0]) * CAP
    before = (
        lax.broadcasted_iota(jnp.int32, (rows, rows), 0) < lax.broadcasted_iota(jnp.int32, (rows, rows), 1)
    ).astype(BF16)
    slot_row = lax.broadcasted_iota(jnp.int32, (span2, rows), 0).astype(F32)

    def run_experts(chunk):
        pairs = [chunk[i:i + 2] for i in range(0, len(chunk), 2)]
        for p, pair in enumerate(pairs):
            for k in range(2):
                gates = jnp.zeros((span2, 1), F32)
                for i, (dz, dy) in enumerate(pair):
                    source = slot(dz, dy)
                    named = (meta[source, 0:8, :] == ids[k]).astype(F32)
                    mine = jnp.sum(named, axis=0, keepdims=True)
                    gate = jnp.sum(named * meta[source, 8:16, :], axis=0, keepdims=True)
                    rank = dot(jnp.broadcast_to(mine, (8, rows)).astype(BF16), before)[0:1, :]
                    place = jnp.where(mine > 0.0, rank + float(i * CAP), -1.0)
                    chosen = (slot_row == place).astype(F32)
                    pmat[p, k * span2:(k + 1) * span2, i * rows:(i + 1) * rows] = chosen.astype(BF16)
                    gates = gates + jnp.sum(chosen * gate, axis=1, keepdims=True)
                gslot[k, p * span2:(p + 1) * span2, :] = jnp.broadcast_to(gates, (span2, HD))
        tile = min(512, width)

        @pl.loop(0, width // tile)
        def _(j):
            cols = pl.ds(pl.multiple_of(j * tile, tile), tile)
            for p, pair in enumerate(pairs):
                joint = jnp.concatenate([tokens[slot(dz, dy), :, cols] for dz, dy in pair], axis=0)
                rows_out = dot(pmat[p], joint).astype(BF16)
                for k in range(2):
                    qrows[k * count + p * span2:k * count + (p + 1) * span2, cols] = rows_out[k * span2:(k + 1) * span2, :]

        tile_f = min(256, inner)

        @pl.loop(0, inner // tile_f)
        def _(j):
            start = pl.multiple_of(j * tile_f, tile_f)
            for k in range(2):
                gate = dot(qrows[k * count:(k + 1) * count, :], up[k, :, pl.ds(start, tile_f)])
                lift = dot(qrows[k * count:(k + 1) * count, :], up[k, :, pl.ds(pl.multiple_of(inner + start, tile_f), tile_f)])
                hid[k, :, pl.ds(start, tile_f)] = (gate / (1.0 + jnp.exp(-gate)) * lift).astype(BF16)

        tile_d = min(256, width)

        @pl.loop(0, width // tile_d)
        def _(j):
            cols = pl.ds(pl.multiple_of(j * tile_d, tile_d), tile_d)
            made = []
            for k in range(2):
                made.append((dot(hid[k], down[k, :, cols]) * gslot[k, :, 0:1]).astype(BF16))
            for p, pair in enumerate(pairs):
                joint = jnp.concatenate([m[p * span2:(p + 1) * span2, :] for m in made], axis=0)
                placed = dot_0(pmat[p], joint).astype(BF16)
                for i, (dz, dy) in enumerate(pair):
                    sums[slot(dz, dy), :, cols] = placed[i * rows:(i + 1) * rows, :]

    def sum_view(h, i, j, start, count):
        dz, dy = (i, j) if h == 0 else (j, i)
        return sums.at[slot(dz, dy), pl.ds(h * half + start, count)]

    first = ((yp, ym), (zp, zm))
    second = ((zp, zm), (yp, ym))

    def far_out(h, i):
        copies.start(("1+", h, i), sum_view(h, i, 2, 0, quarter), r1.at[h, i, pl.ds(0, quarter)], first[h][0])
        copies.start(("1-", h, i), sum_view(h, i, 2, quarter, quarter), r1.at[h, i, pl.ds(quarter, quarter)], first[h][1])

    def add_to(ref, more):
        ref[...] = (ref[...].astype(F32) + more[...].astype(F32)).astype(BF16)

    def near_out(h, i):
        copies.arrived(("1+", h, i))
        add_to(sum_view(h, i, 1, 0, quarter), r1.at[h, i, pl.ds(0, quarter)])
        copies.start(("2+", h, i), sum_view(h, i, 1, 0, half), r2.at[h, i, 0], first[h][0])
        copies.arrived(("1-", h, i))
        add_to(sum_view(h, i, 3, quarter, quarter), r1.at[h, i, pl.ds(quarter, quarter)])
        copies.start(("2-", h, i), sum_view(h, i, 3, 0, half), r2.at[h, i, 1], first[h][1])

    def gathered(h, i, start, count):
        span = pl.ds(start, count)
        return (
            sum_view(h, i, 0, start, count)[...].astype(F32)
            + r2[h, i, 0, span, :].astype(F32)
            + r2[h, i, 1, span, :].astype(F32)
        )

    def arrived_2(h, i):
        copies.arrived(("2+", h, i))
        copies.arrived(("2-", h, i))

    loads["cache"].wait()
    prefix(0, [0])
    q_on(0)
    q_out(1)
    copies.arrived("f1")
    copies.arrived("f3")
    prefix(0, [1, 3])
    direct_out(0)
    copies.arrived(("q2+", 0))
    copies.arrived(("q2-", 0))
    copies.arrived("f2")
    prefix(0, [2])
    relay_out(0)
    for d in (3, 1):
        source = told(d, 0)
        tell(d, 3, source, yp)
        tell(d, 1, source, ym)
        if d == 3:
            tell(2, 0, source, zp)
    prefix(1, [0])
    relay_on(0)
    q_on(1)
    source = told(2, 0)
    tell(2, 3, source, yp)
    tell(2, 1, source, ym)
    prefix(1, [1, 3])
    direct_out(1)
    finish(0)
    spread_0(0)
    for d in range(SIDE):
        tell(d, 2, told(d, 3), yp)
    copies.arrived(("q2+", 1))
    copies.arrived(("q2-", 1))
    prefix(1, [2])
    relay_out(1)
    spread_1(0)
    relay_on(1)
    pass_second(0, 0)
    spread_far(0)
    for d in range(SIDE):
        told(d, 1)
        told(d, 2)
    finish(1)
    spread_0(1)
    pass_second(0, 1)
    pass_second(0, 3)
    spread_1(1)
    pass_second(0, 2)
    pass_second(1, 0)
    for key in ("up", "down"):
        loads[key].wait()
        copies.arrived(key)
    for g in range(GROUPS):
        for key in ("q2+", "q2-", "r_high", "l_low", "relay_r", "relay_l", "r_low", "l_high"):
            copies.left((key, g))

    def run(chunk):
        for dz, dy in chunk:
            for g in range(GROUPS):
                have(("a", g), dz, dy)
                have(("b", g), dz, dy)
        run_experts(chunk)

    run(CHUNKS[0])
    spread_far(1)
    pass_second(1, 1)
    run(CHUNKS[1])
    pass_second(1, 3)
    pass_second(1, 2)
    run(CHUNKS[2])
    for i in (0, 1):
        for h in range(2):
            far_out(h, i)
    run(CHUNKS[3])
    for i in (2, 3):
        for h in range(2):
            far_out(h, i)

    level = part
    lo, hi = pl.ds(0, quarter), pl.ds(quarter, quarter)

    def level_rows(h, start, count):
        return pl.ds(h * half + start, count)

    for i in (2, 1, 3, 0):
        for h in range(2):
            near_out(h, i)
    for h in range(2):
        arrived_2(h, 2)
        level[2, level_rows(h, 0, half), :] = gathered(h, 2, 0, half).astype(BF16)
        copies.start(("3+", h), level.at[2, level_rows(h, 0, quarter)], r3.at[h, lo], second[h][0])
        copies.start(("3-", h), level.at[2, level_rows(h, quarter, quarter)], r3.at[h, hi], second[h][1])
    for h in range(2):
        arrived_2(h, 1)
        copies.arrived(("3+", h))
        level[1, level_rows(h, 0, quarter), :] = (gathered(h, 1, 0, quarter) + r3[h, lo, :].astype(F32)).astype(BF16)
        level[1, level_rows(h, quarter, quarter), :] = gathered(h, 1, quarter, quarter).astype(BF16)
        copies.start(("4+", h), level.at[1, level_rows(h, 0, half)], r4.at[h, 0], second[h][0])
        arrived_2(h, 3)
        copies.arrived(("3-", h))
        level[3, level_rows(h, 0, quarter), :] = gathered(h, 3, 0, quarter).astype(BF16)
        level[3, level_rows(h, quarter, quarter), :] = (gathered(h, 3, quarter, quarter) + r3[h, hi, :].astype(F32)).astype(BF16)
        copies.start(("4-", h), level.at[3, level_rows(h, 0, half)], r4.at[h, 1], second[h][1])
    for h in range(2):
        arrived_2(h, 0)
        copies.arrived(("4+", h))
        copies.arrived(("4-", h))
        span = pl.ds(h * half, half)
        mixture = gathered(h, 0, 0, half) + r4[h, 0].astype(F32) + r4[h, 1].astype(F32)
        position = lax.broadcasted_iota(jnp.int32, (half, width), 0) + h * half
        out_ref[span, :] = jnp.where(position < length, own[span, :] + mixture, 0.0).astype(BF16)
    copies.drain()


def layer(length, group, owner, queries, pairs, cache, weight, hidden, gain, routes, gates, upward, downward):
    rows, width = queries.shape
    heads = width // HD
    inner = downward.shape[0]
    half = rows // 2
    slots = SIDE * SIDE
    count = len(CHUNKS[0]) * CAP
    dma = pltpu.SemaphoreType.DMA
    return pl.pallas_call(
        layer_kernel,
        out_shape=jax.ShapeDtypeStruct((rows, width), BF16),
        in_specs=[SMEM, SMEM, SMEM, VMEM, VMEM, ANY, ANY, VMEM, VMEM, VMEM, VMEM, ANY, ANY],
        out_specs=VMEM,
        scratch_shapes=[
            pltpu.VMEM((3 * rows, width), BF16),
            pltpu.VMEM((8, HD), F32),
            pltpu.VMEM((3, 8, HD), F32),
            pltpu.VMEM(cache.shape, BF16),
            pltpu.VMEM((4, rows, width), BF16),
            pltpu.VMEM((GROUPS, 4, rows, HD), F32),
            pltpu.VMEM((GROUPS, 4, heads, rows), F32),
            pltpu.VMEM((GROUPS, 3, heads, rows), F32),
            pltpu.VMEM((rows, width), F32),
            pltpu.VMEM((rows, HD), F32),
            pltpu.VMEM((GROUPS, 2, rows // GROUPS // 2, width), BF16),
            pltpu.VMEM((2, rows, width), BF16),
            pltpu.VMEM((rows // GROUPS, width), BF16),
            pltpu.VMEM((slots, 16, rows), F32),
            pltpu.VMEM((slots, rows, width), BF16),
            pltpu.VMEM((2,) + upward.shape, BF16),
            pltpu.VMEM((2,) + downward.shape, BF16),
            pltpu.VMEM((len(CHUNKS[0]) // 2, 4 * CAP, 2 * rows), BF16),
            pltpu.VMEM((2, count, HD), F32),
            pltpu.VMEM((2, count, inner), BF16),
            pltpu.VMEM((slots, width // slots, width), BF16),
            pltpu.VMEM((2, SIDE, half, width), BF16),
            pltpu.VMEM((2, SIDE, 2, half, width), BF16),
            pltpu.VMEM((2, half, width), BF16),
            pltpu.VMEM((2, 2, half, width), BF16),
            dma((180,)),
            dma((180,)),
            dma((4,)),
        ],
        compiler_params=pltpu.CompilerParams(
            collective_id=0, has_side_effects=True, vmem_limit_bytes=VMEM_LIMIT
        ),
        name="layer",
    )(
        length, group, owner, queries, pairs, cache, weight.reshape(slots, width // slots, width), hidden, gain,
        routes, gates, upward, downward,
    )


def on_device(
    hidden_in, queries, suffix_pairs, prefix_cache, suffix_length, request_group, prefix_owner,
    out_weight, norm_gain, routes, gate_values, expert_upward, expert_downward,
):
    rows, width = hidden_in.shape[2:]
    out = layer(
        suffix_length, request_group, prefix_owner, queries[0, 0], suffix_pairs[0, 0], prefix_cache[0, 0], out_weight,
        hidden_in[0, 0], norm_gain.reshape(1, width), routes[0, 0], gate_values[0, 0], expert_upward[0], expert_downward[0],
    )
    return out.reshape(1, 1, rows, width)


def solution(mesh):
    in_specs = (
        P("req", "exp", None, None),
        P("req", "exp", None, None),
        P("req", "exp", None, None, None),
        P("exp", "req", None, None, None),
        P("req", "exp"),
        P("req", "exp"),
        P("exp", None),
        P(),
        P(),
        P("req", "exp", None, None),
        P("req", "exp", None, None),
        P("exp", None, None),
        P("exp", None, None),
    )
    out_specs = P("req", "exp", None, None)
    return jax.shard_map(
        on_device, mesh=mesh, in_specs=in_specs, out_specs=out_specs, check_vma=False
    )
```

time: 182 us -> 168 us (0.923)
  Pallas kernels: 175 us -> 162 us
  other arithmetic: 2.63 us -> 0 us
    pallas_call x2 -> x1, Pallas kernels: 175 us -> 162 us  [layer(): pl.pallas_call(layer_kernel, out_shape=jax.ShapeDtypeStruct((rows, width)...]
    unnamed x3, local copies, waits for them, and re-layouts: 1.89 us -> 4.7 us
where the time goes in v2:
time: 168 us
  Pallas kernels  162 us (96%)
  local copies, waits for them, and re-layouts  4.7 us (3%)
    pallas_call x1, Pallas kernels, layer(): pl.pallas_call(layer_kernel, out_shape=jax.ShapeDtypeStruct((rows, width)...  162 us
    unnamed x3, local copies, waits for them, and re-layouts  4.7 us

profile of v2, /device:TPU:0, one launch (start us, length us, event | category | flops | bytes accessed | tf_op | source)
XLA Modules:
  0.0 167.7 jit_solution(8665904462769995366)
XLA Ops:
  1.3 1.4 copy.14
  2.7 1.4 copy.15
  4.1 161.7 %layer.1 = bf16[128,2048]{1,0:T(8,128)(2,1)} custom-call(s32[1,1]{1,0:T(1,128)S(6)} %copy.17.length_ref, s32[1,1]{1,0:T(1,128)S(6)} %copy.18.group_ref, s32[1,4]{1,0:T(1,128)} %owner_ref.1, bf16[128,2048]{1,0:T(8,128)(2,1)} %bitcast.17, bf16[2,128,2048]{2,1,0:T(8,128)(2,1)} %bitcast.16, bf16[2,384,2048]{2,1,0:T(8,128)(2,1)} %bitcast.14, ...), custom_call_target="tpu_custom_call" | custom-call | tf_op jit(solution)/shard_map/layer/pallas_call | solution.py:575
  165.8 1.9 %copy.19 = bf16[1,1,128,2048]{3,2,1,0:T(8,128)(2,1)} copy(bf16[1,1,128,2048]{3,2,1,0:T(8,128)(2,1)} %bitcast.15) | data formatting | bytes 1048576

commit v3 on v2

--- a/solution.py
+++ b/solution.py
@@ -84,9 +84,9 @@
 GROUPS = 2
 CHUNKS = (
     ((0, 0), (0, 1), (0, 3), (1, 0)),
-    ((3, 0), (2, 0), (0, 2), (1, 1)),
-    ((1, 3), (3, 1), (1, 2), (2, 1)),
-    ((3, 3), (3, 2), (2, 3), (2, 2)),
+    ((0, 2), (2, 0), (1, 2), (2, 1)),
+    ((2, 2), (3, 2), (2, 3), (3, 0)),
+    ((1, 1), (1, 3), (3, 1), (3, 3)),
 )
 
 
@@ -196,19 +196,21 @@
 
     own_c = lax.broadcasted_iota(jnp.int32, (rows, rows), 1)
     own_t = lax.broadcasted_iota(jnp.int32, (rows, rows), 0)
-    several = min(2, heads)
-
-    @pl.loop(0, heads // several)
-    def _(block):
-        stats = own_stat[...]
-        for k in range(several):
-            h = block * several + k
-            cols = columns(h)
-            scores = dot_t(q_ref[:, cols], pairs_ref[0, :, cols]) * scale
-            out, lse = softmax(scores, own_c <= own_t, pairs_ref[1, :, cols])
-            own[:, cols] = out
-            stats = jnp.where(lane == h, lse, stats)
-        own_stat[...] = stats
+
+    def own_part():
+        several = min(2, heads)
+
+        @pl.loop(0, heads // several)
+        def _(block):
+            stats = own_stat[...]
+            for k in range(several):
+                h = block * several + k
+                cols = columns(h)
+                scores = dot_t(q_ref[:, cols], pairs_ref[0, :, cols]) * scale
+                out, lse = softmax(scores, own_c <= own_t, pairs_ref[1, :, cols])
+                own[:, cols] = out
+                stats = jnp.where(lane == h, lse, stats)
+            own_stat[...] = stats
 
     def prefix(g, slots):
         c = lax.broadcasted_iota(jnp.int32, (size, window), 1)
@@ -452,8 +454,8 @@
 
     loads["cache"].wait()
     prefix(0, [0])
+    own_part()
     q_on(0)
-    q_out(1)
     copies.arrived("f1")
     copies.arrived("f3")
     prefix(0, [1, 3])
@@ -463,42 +465,43 @@
     copies.arrived("f2")
     prefix(0, [2])
     relay_out(0)
+    q_out(1)
+    prefix(1, [0])
+    relay_on(0)
     for d in (3, 1):
         source = told(d, 0)
         tell(d, 3, source, yp)
         tell(d, 1, source, ym)
         if d == 3:
             tell(2, 0, source, zp)
-    prefix(1, [0])
-    relay_on(0)
     q_on(1)
-    source = told(2, 0)
-    tell(2, 3, source, yp)
-    tell(2, 1, source, ym)
+    finish(0)
+    spread_0(0)
     prefix(1, [1, 3])
     direct_out(1)
-    finish(0)
-    spread_0(0)
-    for d in range(SIDE):
-        tell(d, 2, told(d, 3), yp)
+    spread_1(0)
     copies.arrived(("q2+", 1))
     copies.arrived(("q2-", 1))
     prefix(1, [2])
     relay_out(1)
-    spread_1(0)
+    source = told(2, 0)
+    tell(2, 3, source, yp)
+    tell(2, 1, source, ym)
+    pass_second(0, 0)
     relay_on(1)
-    pass_second(0, 0)
     spread_far(0)
-    for d in range(SIDE):
-        told(d, 1)
-        told(d, 2)
     finish(1)
     spread_0(1)
+    for d in range(SIDE):
+        tell(d, 2, told(d, 3), yp)
     pass_second(0, 1)
     pass_second(0, 3)
     spread_1(1)
     pass_second(0, 2)
     pass_second(1, 0)
+    for d in range(SIDE):
+        told(d, 1)
+        told(d, 2)
     for key in ("up", "down"):
         loads[key].wait()
         copies.arrived(key)
@@ -513,35 +516,38 @@
                 have(("b", g), dz, dy)
         run_experts(chunk)
 
-    run(CHUNKS[0])
-    spread_far(1)
-    pass_second(1, 1)
-    run(CHUNKS[1])
-    pass_second(1, 3)
-    pass_second(1, 2)
-    run(CHUNKS[2])
-    for i in (0, 1):
-        for h in range(2):
-            far_out(h, i)
-    run(CHUNKS[3])
-    for i in (2, 3):
-        for h in range(2):
-            far_out(h, i)
-
     level = part
     lo, hi = pl.ds(0, quarter), pl.ds(quarter, quarter)
 
     def level_rows(h, start, count):
         return pl.ds(h * half + start, count)
 
-    for i in (2, 1, 3, 0):
-        for h in range(2):
-            near_out(h, i)
-    for h in range(2):
+    def level_far(h):
         arrived_2(h, 2)
         level[2, level_rows(h, 0, half), :] = gathered(h, 2, 0, half).astype(BF16)
         copies.start(("3+", h), level.at[2, level_rows(h, 0, quarter)], r3.at[h, lo], second[h][0])
         copies.start(("3-", h), level.at[2, level_rows(h, quarter, quarter)], r3.at[h, hi], second[h][1])
+
+    run(CHUNKS[0])
+    spread_far(1)
+    pass_second(1, 1)
+    pass_second(1, 3)
+    pass_second(1, 2)
+    run(CHUNKS[1])
+    for h, i in ((0, 0), (1, 0), (0, 1), (1, 1)):
+        far_out(h, i)
+    run(CHUNKS[2])
+    for h, i in ((0, 2), (1, 2), (0, 3), (1, 3)):
+        far_out(h, i)
+    for h, i in ((0, 0), (1, 0)):
+        near_out(h, i)
+    run(CHUNKS[3])
+    for h, i in ((0, 2), (1, 2), (0, 1), (1, 1)):
+        near_out(h, i)
+    level_far(0)
+    level_far(1)
+    for h, i in ((0, 3), (1, 3)):
+        near_out(h, i)
     for h in range(2):
         arrived_2(h, 1)
         copies.arrived(("3+", h))

time: 168 us -> 168 us (level)
  Pallas kernels: 162 us -> 160 us
where the time goes in v3:
time: 168 us; the launch traced here: 166 us
  Pallas kernels  160 us (95%)
  local copies, waits for them, and re-layouts  4.7 us (3%)
    pallas_call x1, Pallas kernels, layer(): pl.pallas_call(layer_kernel, out_shape=jax.ShapeDtypeStruct((rows, width)...  160 us
    unnamed x3, local copies, waits for them, and re-layouts  4.7 us

profile of v3, /device:TPU:0, one launch (start us, length us, event | category | flops | bytes accessed | tf_op | source)
XLA Modules:
  0.0 166.5 jit_solution(3486760087406142676)
XLA Ops:
  1.3 1.4 copy.14
  2.7 1.4 copy.15
  4.1 160.4 %layer.1 = bf16[128,2048]{1,0:T(8,128)(2,1)} custom-call(s32[1,1]{1,0:T(1,128)S(6)} %copy.17.length_ref, s32[1,1]{1,0:T(1,128)S(6)} %copy.18.group_ref, s32[1,4]{1,0:T(1,128)} %owner_ref.1, bf16[128,2048]{1,0:T(8,128)(2,1)} %bitcast.17, bf16[2,128,2048]{2,1,0:T(8,128)(2,1)} %bitcast.16, bf16[2,384,2048]{2,1,0:T(8,128)(2,1)} %bitcast.14, ...), custom_call_target="tpu_custom_call" | custom-call | tf_op jit(solution)/shard_map/layer/pallas_call | solution.py:581
  164.6 1.9 %copy.19 = bf16[1,1,128,2048]{3,2,1,0:T(8,128)(2,1)} copy(bf16[1,1,128,2048]{3,2,1,0:T(8,128)(2,1)} %bitcast.15) | data formatting | bytes 1048576

commit v4 on v3

--- a/solution.py
+++ b/solution.py
@@ -29,10 +29,6 @@
     return jnp.dot(a, b, preferred_element_type=F32)
 
 
-def dot_0(a, b):
-    return lax.dot_general(a, b, (((0,), (0,)), ((), ())), preferred_element_type=F32)
-
-
 class Copies:
     def __init__(self, send, recv):
         self.send, self.recv, self.made, self.gone = send, recv, {}, set()
@@ -82,6 +78,7 @@
 
 
 GROUPS = 2
+LOG2E = 1.4426950408889634
 CHUNKS = (
     ((0, 0), (0, 1), (0, 3), (1, 0)),
     ((0, 2), (2, 0), (1, 2), (2, 1)),
@@ -99,7 +96,7 @@
     routes_ref, gates_ref, up_ref, down_ref,
     out_ref,
     qrows, flag, flags, cache, part, stat, stat_t, stat_in, own, own_stat, relay, back, attn,
-    meta, tokens, up, down, pmat, gslot, hid, sums, r1, r2, r3, r4,
+    bias, meta, tokens, up, down, pmat, pmat_t, gslot, hid, sums, r1, r2, r3, r4,
     send, recv, local,
 ):
     x, e = lax.axis_index("req"), lax.axis_index("exp")
@@ -184,12 +181,22 @@
     stat[...] = jnp.zeros_like(stat)
     own_stat[...] = jnp.zeros_like(own_stat)
 
-    def softmax(scores, visible, values):
-        masked = jnp.where(visible, scores, NEG)
+    def softmax(masked):
         largest = jnp.max(masked, axis=1, keepdims=True)
-        weights = jnp.exp(masked - largest)
+        weights = jnp.exp2((masked - largest) * (scale * LOG2E))
         totals = jnp.sum(weights, axis=1, keepdims=True)
-        return dot(weights.astype(BF16), values) * (1.0 / totals), largest + jnp.log(totals)
+        return weights.astype(BF16), 1.0 / totals, largest * scale + jnp.log(totals)
+
+    def in_turn(jobs, scores, values, store):
+        made, soft = {}, {}
+        for step in range(len(jobs) + 2):
+            if step < len(jobs):
+                made[step] = scores(jobs[step])
+            if 0 <= step - 1 < len(jobs):
+                soft[step - 1] = softmax(made.pop(step - 1))
+            if step >= 2:
+                weights, inverse, lse = soft.pop(step - 2)
+                store(jobs[step - 2], dot(weights, values(jobs[step - 2])) * inverse, lse)
 
     def columns(h):
         return pl.ds(pl.multiple_of(h * HD, HD), HD)
@@ -198,39 +205,56 @@
     own_t = lax.broadcasted_iota(jnp.int32, (rows, rows), 0)
 
     def own_part():
-        several = min(2, heads)
+        several = min(4, heads)
+        own_bias = jnp.where(own_c <= own_t, 0.0, NEG)
 
         @pl.loop(0, heads // several)
         def _(block):
-            stats = own_stat[...]
-            for k in range(several):
-                h = block * several + k
-                cols = columns(h)
-                scores = dot_t(q_ref[:, cols], pairs_ref[0, :, cols]) * scale
-                out, lse = softmax(scores, own_c <= own_t, pairs_ref[1, :, cols])
-                own[:, cols] = out
-                stats = jnp.where(lane == h, lse, stats)
-            own_stat[...] = stats
-
-    def prefix(g, slots):
+            stats = [own_stat[...]]
+
+            def scores(k):
+                cols = columns(block * several + k)
+                return dot_t(q_ref[:, cols], pairs_ref[0, :, cols]) + own_bias
+
+            def store(k, out, lse):
+                own[:, columns(block * several + k)] = out
+                stats[0] = jnp.where(lane == block * several + k, lse, stats[0])
+
+            in_turn(
+                list(range(several)), scores, lambda k: pairs_ref[1, :, columns(block * several + k)], store
+            )
+            own_stat[...] = stats[0]
+
+    for g in range(GROUPS):
         c = lax.broadcasted_iota(jnp.int32, (size, window), 1)
         t = lax.broadcasted_iota(jnp.int32, (size, window), 0) + g * size
-        visible = (c < SINK) | (c > t)
+        bias[g] = jnp.where((c < SINK) | (c > t), 0.0, NEG)
+
+    def prefix(g, slots):
         span = rows_of(g)
         valid = {d: (flag if d == 0 else flags.at[d - 1])[pl.ds(x, 1), :] for d in slots}
-        several = min(4 // len(slots), heads)
+        several = min(8 // len(slots), heads)
 
         @pl.loop(0, heads // several)
         def _(block):
             stats = {d: stat[g, d, 0:size, :] for d in slots}
-            for k in range(several):
+
+            def scores(job):
+                k, d = job
+                cols = columns(block * several + k)
+                q = q_ref[span, cols] if d == 0 else q_slot(d, span)[:, cols]
+                return dot_t(q, cache[0, :, cols]) + bias[g]
+
+            def store(job, out, lse):
+                k, d = job
                 h = block * several + k
-                cols = columns(h)
-                for d in slots:
-                    q = q_ref[span, cols] if d == 0 else q_slot(d, span)[:, cols]
-                    out, lse = softmax(dot_t(q, cache[0, :, cols]) * scale, visible, cache[1, :, cols])
-                    part[d, span, cols] = (out * valid[d]).astype(BF16)
-                    stats[d] = jnp.where(lane_g == h, lse * valid[d], stats[d])
+                part[d, span, columns(h)] = (out * valid[d]).astype(BF16)
+                stats[d] = jnp.where(lane_g == h, lse * valid[d], stats[d])
+
+            in_turn(
+                [(k, d) for k in range(several) for d in slots], scores,
+                lambda job: cache[1, :, columns(block * several + job[0])], store,
+            )
             for d in slots:
                 stat[g, d, 0:size, :] = stats[d]
 
@@ -259,7 +283,7 @@
         part[3, high, :] = part[3, high, :] + relay[g, 1]
         copies.start(("l_high", g), part.at[3, high], back.at[1, high], left)
 
-    tile = min(256, width)
+    tile = min(512, width)
 
     def finish(g):
         for key in ("s1", "s2", "s3", "r_high", "l_low", "r_low", "l_high"):
@@ -370,19 +394,24 @@
     def run_experts(chunk):
         pairs = [chunk[i:i + 2] for i in range(0, len(chunk), 2)]
         for p, pair in enumerate(pairs):
-            for k in range(2):
-                gates = jnp.zeros((span2, 1), F32)
-                for i, (dz, dy) in enumerate(pair):
-                    source = slot(dz, dy)
+            gates = [jnp.zeros((span2, 1), F32)] * 2
+            for i, (dz, dy) in enumerate(pair):
+                source = slot(dz, dy)
+                both_chosen = []
+                for k in range(2):
                     named = (meta[source, 0:8, :] == ids[k]).astype(F32)
                     mine = jnp.sum(named, axis=0, keepdims=True)
                     gate = jnp.sum(named * meta[source, 8:16, :], axis=0, keepdims=True)
                     rank = dot(jnp.broadcast_to(mine, (8, rows)).astype(BF16), before)[0:1, :]
                     place = jnp.where(mine > 0.0, rank + float(i * CAP), -1.0)
                     chosen = (slot_row == place).astype(F32)
-                    pmat[p, k * span2:(k + 1) * span2, i * rows:(i + 1) * rows] = chosen.astype(BF16)
-                    gates = gates + jnp.sum(chosen * gate, axis=1, keepdims=True)
-                gslot[k, p * span2:(p + 1) * span2, :] = jnp.broadcast_to(gates, (span2, HD))
+                    gates[k] = gates[k] + jnp.sum(chosen * gate, axis=1, keepdims=True)
+                    both_chosen.append(chosen)
+                chosen = jnp.concatenate(both_chosen, axis=0)
+                pmat[p, :, i * rows:(i + 1) * rows] = chosen.astype(BF16)
+                pmat_t[p, i * rows:(i + 1) * rows, :] = jnp.transpose(chosen).astype(BF16)
+            for k in range(2):
+                gslot[k, p * span2:(p + 1) * span2, :] = jnp.broadcast_to(gates[k], (span2, HD))
         tile = min(512, width)
 
         @pl.loop(0, width // tile)
@@ -405,18 +434,23 @@
                 hid[k, :, pl.ds(start, tile_f)] = (gate / (1.0 + jnp.exp(-gate)) * lift).astype(BF16)
 
         tile_d = min(256, width)
-
-        @pl.loop(0, width // tile_d)
-        def _(j):
-            cols = pl.ds(pl.multiple_of(j * tile_d, tile_d), tile_d)
-            made = []
-            for k in range(2):
-                made.append((dot(hid[k], down[k, :, cols]) * gslot[k, :, 0:1]).astype(BF16))
-            for p, pair in enumerate(pairs):
-                joint = jnp.concatenate([m[p * span2:(p + 1) * span2, :] for m in made], axis=0)
-                placed = dot_0(pmat[p], joint).astype(BF16)
-                for i, (dz, dy) in enumerate(pair):
-                    sums[slot(dz, dy), :, cols] = placed[i * rows:(i + 1) * rows, :]
+        turns = min(2, width // tile_d)
+
+        @pl.loop(0, width // (turns * tile_d))
+        def _(block):
+            joint = []
+            for turn in range(turns):
+                cols = pl.ds(pl.multiple_of((block * turns + turn) * tile_d, tile_d), tile_d)
+                made = [(dot(hid[k], down[k, :, cols]) * gslot[k, :, 0:1]).astype(BF16) for k in range(2)]
+                joint.append([
+                    jnp.concatenate([m[p * span2:(p + 1) * span2, :] for m in made], axis=0) for p in range(len(pairs))
+                ])
+            for turn in range(turns):
+                cols = pl.ds(pl.multiple_of((block * turns + turn) * tile_d, tile_d), tile_d)
+                for p, pair in enumerate(pairs):
+                    placed = dot(pmat_t[p], joint[turn][p]).astype(BF16)
+                    for i, (dz, dy) in enumerate(pair):
+                        sums[slot(dz, dy), :, cols] = placed[i * rows:(i + 1) * rows, :]
 
     def sum_view(h, i, j, start, count):
         dz, dy = (i, j) if h == 0 else (j, i)
@@ -597,11 +631,13 @@
             pltpu.VMEM((GROUPS, 2, rows // GROUPS // 2, width), BF16),
             pltpu.VMEM((2, rows, width), BF16),
             pltpu.VMEM((rows // GROUPS, width), BF16),
+            pltpu.VMEM((GROUPS, rows // GROUPS, cache.shape[1]), F32),
             pltpu.VMEM((slots, 16, rows), F32),
             pltpu.VMEM((slots, rows, width), BF16),
             pltpu.VMEM((2,) + upward.shape, BF16),
             pltpu.VMEM((2,) + downward.shape, BF16),
             pltpu.VMEM((len(CHUNKS[0]) // 2, 4 * CAP, 2 * rows), BF16),
+            pltpu.VMEM((len(CHUNKS[0]) // 2, 2 * rows, 4 * CAP), BF16),
             pltpu.VMEM((2, count, HD), F32),
             pltpu.VMEM((2, count, inner), BF16),
             pltpu.VMEM((slots, width // slots, width), BF16),

time: 168 us -> 148 us (0.88)
  Pallas kernels: 160 us -> 142 us
    pallas_call x1, Pallas kernels: 160 us -> 142 us  [layer(): pl.pallas_call(layer_kernel, out_shape=jax.ShapeDtypeStruct((rows, width)...]
where the time goes in v4:
time: 148 us
  Pallas kernels  142 us (96%)
  local copies, waits for them, and re-layouts  4.7 us (3%)
    pallas_call x1, Pallas kernels, layer(): pl.pallas_call(layer_kernel, out_shape=jax.ShapeDtypeStruct((rows, width)...  142 us
    unnamed x3, local copies, waits for them, and re-layouts  4.7 us

profile of v4, /device:TPU:0, one launch (start us, length us, event | category | flops | bytes accessed | tf_op | source)
XLA Modules:
  0.0 147.5 jit_solution(9138695370228221462)
XLA Ops:
  1.3 1.4 copy.14
  2.7 1.4 copy.15
  4.1 141.5 %layer.1 = bf16[128,2048]{1,0:T(8,128)(2,1)} custom-call(s32[1,1]{1,0:T(1,128)S(6)} %copy.17.length_ref, s32[1,1]{1,0:T(1,128)S(6)} %copy.18.group_ref, s32[1,4]{1,0:T(1,128)} %owner_ref.1, bf16[128,2048]{1,0:T(8,128)(2,1)} %bitcast.17, bf16[2,128,2048]{2,1,0:T(8,128)(2,1)} %bitcast.16, bf16[2,384,2048]{2,1,0:T(8,128)(2,1)} %bitcast.14, ...), custom_call_target="tpu_custom_call" | custom-call | tf_op jit(solution)/shard_map/layer/pallas_call | solution.py:615
  145.7 1.9 %copy.19 = bf16[1,1,128,2048]{3,2,1,0:T(8,128)(2,1)} copy(bf16[1,1,128,2048]{3,2,1,0:T(8,128)(2,1)} %bitcast.15) | data formatting | bytes 1048576

commit v5 on v4

--- a/solution.py
+++ b/solution.py
@@ -81,9 +81,10 @@
 LOG2E = 1.4426950408889634
 CHUNKS = (
     ((0, 0), (0, 1), (0, 3), (1, 0)),
-    ((0, 2), (2, 0), (1, 2), (2, 1)),
-    ((2, 2), (3, 2), (2, 3), (3, 0)),
-    ((1, 1), (1, 3), (3, 1), (3, 3)),
+    ((0, 2), (2, 0)),
+    ((1, 2), (2, 1), (3, 0), (1, 1)),
+    ((2, 2), (3, 2), (2, 3), (1, 3)),
+    ((3, 1), (3, 3)),
 )
 
 
@@ -145,18 +146,31 @@
     def q_slot(d, span):
         return qrows.at[pl.ds((d - 1) * rows + span.start, span.size)]
 
-    def q_out(g):
-        copies.start(("q", 3, g), q_ref.at[rows_of(g)], q_slot(3, rows_of(g)), right)
-        copies.start(("q", 1, g), q_ref.at[rows_of(g)], q_slot(1, rows_of(g)), left)
+    def q_piece(g, hop, piece):
+        span = rows_of(g, piece * part_half, part_half)
+        copies.start(("q", hop, g, piece), q_ref.at[span], q_slot(hop, span), right if hop == 3 else left)
+
+    def q_first(g):
+        q_piece(g, 3, 0)
+        q_piece(g, 1, 1)
+
+    def q_rest(g):
+        q_piece(g, 3, 1)
+        q_piece(g, 1, 0)
 
     def q_on(g):
         low, high = rows_of(g, 0, part_half), rows_of(g, part_half, part_half)
-        copies.arrived(("q", 3, g))
+        copies.arrived(("q", 3, g, 0))
         copies.start(("q2+", g), q_slot(3, low), q_slot(2, low), right)
-        copies.arrived(("q", 1, g))
+        copies.arrived(("q", 1, g, 1))
         copies.start(("q2-", g), q_slot(1, high), q_slot(2, high), left)
 
-    q_out(0)
+    def q_near(g):
+        copies.arrived(("q", 3, g, 1))
+        copies.arrived(("q", 1, g, 0))
+
+    q_first(0)
+    q_rest(0)
     copies.start("f3", flag, flags.at[2], right)
     copies.start("f1", flag, flags.at[0], left)
     copies.start("f2", flag, flags.at[1], across)
@@ -393,6 +407,7 @@
 
     def run_experts(chunk):
         pairs = [chunk[i:i + 2] for i in range(0, len(chunk), 2)]
+        held = len(chunk) * CAP
         for p, pair in enumerate(pairs):
             gates = [jnp.zeros((span2, 1), F32)] * 2
             for i, (dz, dy) in enumerate(pair):
@@ -429,9 +444,9 @@
         def _(j):
             start = pl.multiple_of(j * tile_f, tile_f)
             for k in range(2):
-                gate = dot(qrows[k * count:(k + 1) * count, :], up[k, :, pl.ds(start, tile_f)])
-                lift = dot(qrows[k * count:(k + 1) * count, :], up[k, :, pl.ds(pl.multiple_of(inner + start, tile_f), tile_f)])
-                hid[k, :, pl.ds(start, tile_f)] = (gate / (1.0 + jnp.exp(-gate)) * lift).astype(BF16)
+                gate = dot(qrows[k * count:k * count + held, :], up[k, :, pl.ds(start, tile_f)])
+                lift = dot(qrows[k * count:k * count + held, :], up[k, :, pl.ds(pl.multiple_of(inner + start, tile_f), tile_f)])
+                hid[k, 0:held, pl.ds(start, tile_f)] = (gate / (1.0 + jnp.exp(-gate)) * lift).astype(BF16)
 
         tile_d = min(256, width)
         turns = min(2, width // tile_d)
@@ -441,7 +456,7 @@
             joint = []
             for turn in range(turns):
                 cols = pl.ds(pl.multiple_of((block * turns + turn) * tile_d, tile_d), tile_d)
-                made = [(dot(hid[k], down[k, :, cols]) * gslot[k, :, 0:1]).astype(BF16) for k in range(2)]
+                made = [(dot(hid[k, 0:held, :], down[k, :, cols]) * gslot[k, 0:held, 0:1]).astype(BF16) for k in range(2)]
                 joint.append([
                     jnp.concatenate([m[p * span2:(p + 1) * span2, :] for m in made], axis=0) for p in range(len(pairs))
                 ])
@@ -488,20 +503,22 @@
 
     loads["cache"].wait()
     prefix(0, [0])
+    q_on(0)
     own_part()
-    q_on(0)
     copies.arrived("f1")
     copies.arrived("f3")
+    q_near(0)
     prefix(0, [1, 3])
     direct_out(0)
+    q_first(1)
     copies.arrived(("q2+", 0))
     copies.arrived(("q2-", 0))
     copies.arrived("f2")
     prefix(0, [2])
     relay_out(0)
-    q_out(1)
     prefix(1, [0])
     relay_on(0)
+    q_rest(1)
     for d in (3, 1):
         source = told(d, 0)
         tell(d, 3, source, yp)
@@ -511,6 +528,7 @@
     q_on(1)
     finish(0)
     spread_0(0)
+    q_near(1)
     prefix(1, [1, 3])
     direct_out(1)
     spread_1(0)
@@ -566,16 +584,19 @@
     spread_far(1)
     pass_second(1, 1)
     pass_second(1, 3)
+    run(CHUNKS[1])
     pass_second(1, 2)
-    run(CHUNKS[1])
-    for h, i in ((0, 0), (1, 0), (0, 1), (1, 1)):
+    for h, i in ((0, 0), (1, 0)):
         far_out(h, i)
     run(CHUNKS[2])
-    for h, i in ((0, 2), (1, 2), (0, 3), (1, 3)):
+    for h, i in ((0, 1), (1, 1)):
         far_out(h, i)
     for h, i in ((0, 0), (1, 0)):
         near_out(h, i)
     run(CHUNKS[3])
+    for h, i in ((0, 2), (1, 2), (0, 3), (1, 3)):
+        far_out(h, i)
+    run(CHUNKS[4])
     for h, i in ((0, 2), (1, 2), (0, 1), (1, 1)):
         near_out(h, i)
     level_far(0)

time: 148 us -> 147 us (level)
  no operation moved by 1% of the time
where the time goes in v5:
time: 147 us
  Pallas kernels  141 us (96%)
  local copies, waits for them, and re-layouts  4.7 us (3%)
    pallas_call x1, Pallas kernels, layer(): pl.pallas_call(layer_kernel, out_shape=jax.ShapeDtypeStruct((rows, width)...  141 us
    unnamed x3, local copies, waits for them, and re-layouts  4.7 us

profile of v5, /device:TPU:0, one launch (start us, length us, event | category | flops | bytes accessed | tf_op | source)
XLA Modules:
  0.0 146.5 jit_solution(8837511478439296633)
XLA Ops:
  1.3 1.4 copy.14
  2.7 1.4 copy.15
  4.1 140.5 %layer.1 = bf16[128,2048]{1,0:T(8,128)(2,1)} custom-call(s32[1,1]{1,0:T(1,128)S(6)} %copy.17.length_ref, s32[1,1]{1,0:T(1,128)S(6)} %copy.18.group_ref, s32[1,4]{1,0:T(1,128)} %owner_ref.1, bf16[128,2048]{1,0:T(8,128)(2,1)} %bitcast.17, bf16[2,128,2048]{2,1,0:T(8,128)(2,1)} %bitcast.16, bf16[2,384,2048]{2,1,0:T(8,128)(2,1)} %bitcast.14, ...), custom_call_target="tpu_custom_call" | custom-call | tf_op jit(solution)/shard_map/layer/pallas_call | solution.py:636
  144.6 1.9 %copy.19 = bf16[1,1,128,2048]{3,2,1,0:T(8,128)(2,1)} copy(bf16[1,1,128,2048]{3,2,1,0:T(8,128)(2,1)} %bitcast.15) | data formatting | bytes 1048576

commit v6 on v5

--- a/solution.py
+++ b/solution.py
@@ -13,7 +13,7 @@
 CAP = 40
 NEG = -1e30
 MESH = pl.DeviceIdType.MESH
-VMEM_LIMIT = 63 * 1024 * 1024
+VMEM_LIMIT = 67043328
 F32 = jnp.float32
 BF16 = jnp.bfloat16
 ANY = pl.BlockSpec(memory_space=pl.ANY)
@@ -273,7 +273,7 @@
                 stat[g, d, 0:size, :] = stats[d]
 
         for d in slots:
-            stat_t[g, d] = jnp.transpose(stat[g, d])[0:heads, :]
+            stat_t[g, d] = jnp.transpose(jnp.concatenate([stat[g, d], jnp.zeros((rows - size, HD), F32)], axis=0))[0:heads, :]
 
     def direct_out(g):
         low, high = rows_of(g, 0, part_half), rows_of(g, part_half, part_half)
@@ -304,7 +304,7 @@
             copies.arrived((key, g))
         span = rows_of(g)
         total_t = stat_t[g, 0] + stat_in[g, 0] + stat_in[g, 1] + stat_in[g, 2]
-        stat[g, 0] = jnp.transpose(jnp.concatenate([total_t, jnp.zeros((HD - heads, rows), F32)], axis=0))
+        stat[g, 0] = jnp.transpose(jnp.concatenate([total_t, jnp.zeros((HD - heads, rows), F32)], axis=0))[0:size, :]
         several = min(4, heads)
 
         @pl.loop(0, heads // several)
@@ -405,10 +405,13 @@
     ).astype(BF16)
     slot_row = lax.broadcasted_iota(jnp.int32, (span2, rows), 0).astype(F32)
 
-    def run_experts(chunk):
-        pairs = [chunk[i:i + 2] for i in range(0, len(chunk), 2)]
-        held = len(chunk) * CAP
-        for p, pair in enumerate(pairs):
+    pairs_of, total = {}, 0
+    for chunk in CHUNKS:
+        pairs_of[chunk] = [(total + i // 2, chunk[i:i + 2]) for i in range(0, len(chunk), 2)]
+        total += len(chunk) // 2
+
+    def place_tokens(chunk):
+        for p, pair in pairs_of[chunk]:
             gates = [jnp.zeros((span2, 1), F32)] * 2
             for i, (dz, dy) in enumerate(pair):
                 source = slot(dz, dy)
@@ -426,17 +429,19 @@
                 pmat[p, :, i * rows:(i + 1) * rows] = chosen.astype(BF16)
                 pmat_t[p, i * rows:(i + 1) * rows, :] = jnp.transpose(chosen).astype(BF16)
             for k in range(2):
-                gslot[k, p * span2:(p + 1) * span2, :] = jnp.broadcast_to(gates[k], (span2, HD))
-        tile = min(512, width)
-
-        @pl.loop(0, width // tile)
-        def _(j):
-            cols = pl.ds(pl.multiple_of(j * tile, tile), tile)
-            for p, pair in enumerate(pairs):
+                gslot[:, 2 * p + k:2 * p + k + 1] = gates[k]
+
+    def run_experts(chunk):
+        pairs = pairs_of[chunk]
+        held = len(chunk) * CAP
+        tile = min(1024, width)
+        for start in range(0, width, tile):
+            cols = pl.ds(start, tile)
+            for n, (p, pair) in enumerate(pairs):
                 joint = jnp.concatenate([tokens[slot(dz, dy), :, cols] for dz, dy in pair], axis=0)
                 rows_out = dot(pmat[p], joint).astype(BF16)
                 for k in range(2):
-                    qrows[k * count + p * span2:k * count + (p + 1) * span2, cols] = rows_out[k * span2:(k + 1) * span2, :]
+                    qrows[k * count + n * span2:k * count + (n + 1) * span2, cols] = rows_out[k * span2:(k + 1) * span2, :]
 
         tile_f = min(256, inner)
 
@@ -456,14 +461,17 @@
             joint = []
             for turn in range(turns):
                 cols = pl.ds(pl.multiple_of((block * turns + turn) * tile_d, tile_d), tile_d)
-                made = [(dot(hid[k, 0:held, :], down[k, :, cols]) * gslot[k, 0:held, 0:1]).astype(BF16) for k in range(2)]
+                made = []
+                for k in range(2):
+                    gates = jnp.concatenate([gslot[:, 2 * p + k:2 * p + k + 1] for p, _ in pairs], axis=0)
+                    made.append((dot(hid[k, 0:held, :], down[k, :, cols]) * gates).astype(BF16))
                 joint.append([
-                    jnp.concatenate([m[p * span2:(p + 1) * span2, :] for m in made], axis=0) for p in range(len(pairs))
+                    jnp.concatenate([m[n * span2:(n + 1) * span2, :] for m in made], axis=0) for n in range(len(pairs))
                 ])
             for turn in range(turns):
                 cols = pl.ds(pl.multiple_of((block * turns + turn) * tile_d, tile_d), tile_d)
-                for p, pair in enumerate(pairs):
-                    placed = dot(pmat_t[p], joint[turn][p]).astype(BF16)
+                for n, (p, pair) in enumerate(pairs):
+                    placed = dot(pmat_t[p], joint[turn][n]).astype(BF16)
                     for i, (dz, dy) in enumerate(pair):
                         sums[slot(dz, dy), :, cols] = placed[i * rows:(i + 1) * rows, :]
 
@@ -510,12 +518,12 @@
     q_near(0)
     prefix(0, [1, 3])
     direct_out(0)
-    q_first(1)
     copies.arrived(("q2+", 0))
     copies.arrived(("q2-", 0))
     copies.arrived("f2")
     prefix(0, [2])
     relay_out(0)
+    q_first(1)
     prefix(1, [0])
     relay_on(0)
     q_rest(1)
@@ -542,18 +550,23 @@
     pass_second(0, 0)
     relay_on(1)
     spread_far(0)
+    for d in range(SIDE):
+        tell(d, 2, told(d, 3), yp)
     finish(1)
     spread_0(1)
-    for d in range(SIDE):
-        tell(d, 2, told(d, 3), yp)
     pass_second(0, 1)
     pass_second(0, 3)
-    spread_1(1)
-    pass_second(0, 2)
-    pass_second(1, 0)
     for d in range(SIDE):
         told(d, 1)
         told(d, 2)
+    place_tokens(CHUNKS[0])
+    place_tokens(CHUNKS[1])
+    place_tokens(CHUNKS[2])
+    spread_1(1)
+    pass_second(0, 2)
+    place_tokens(CHUNKS[3])
+    place_tokens(CHUNKS[4])
+    pass_second(1, 0)
     for key in ("up", "down"):
         loads[key].wait()
         copies.arrived(key)
@@ -644,7 +657,7 @@
             pltpu.VMEM((3, 8, HD), F32),
             pltpu.VMEM(cache.shape, BF16),
             pltpu.VMEM((4, rows, width), BF16),
-            pltpu.VMEM((GROUPS, 4, rows, HD), F32),
+            pltpu.VMEM((GROUPS, 4, rows // GROUPS, HD), F32),
             pltpu.VMEM((GROUPS, 4, heads, rows), F32),
             pltpu.VMEM((GROUPS, 3, heads, rows), F32),
             pltpu.VMEM((rows, width), F32),
@@ -657,9 +670,9 @@
             pltpu.VMEM((slots, rows, width), BF16),
             pltpu.VMEM((2,) + upward.shape, BF16),
             pltpu.VMEM((2,) + downward.shape, BF16),
-            pltpu.VMEM((len(CHUNKS[0]) // 2, 4 * CAP, 2 * rows), BF16),
-            pltpu.VMEM((len(CHUNKS[0]) // 2, 2 * rows, 4 * CAP), BF16),
-            pltpu.VMEM((2, count, HD), F32),
+            pltpu.VMEM((slots // 2, 4 * CAP, 2 * rows), BF16),
+            pltpu.VMEM((slots // 2, 2 * rows, 4 * CAP), BF16),
+            pltpu.VMEM((2 * CAP, HD), F32),
             pltpu.VMEM((2, count, inner), BF16),
             pltpu.VMEM((slots, width // slots, width), BF16),
             pltpu.VMEM((2, SIDE, half, width), BF16),

time: 147 us -> 143 us (0.973)
  Pallas kernels: 141 us -> 136 us
    pallas_call x1, Pallas kernels: 141 us -> 136 us  [layer(): pl.pallas_call(layer_kernel, out_shape=jax.ShapeDtypeStruct((rows, width)...]
where the time goes in v6:
time: 143 us; the launch traced here: 142 us
  Pallas kernels  136 us (95%)
  local copies, waits for them, and re-layouts  4.7 us (3%)
    pallas_call x1, Pallas kernels, layer(): pl.pallas_call(layer_kernel, out_shape=jax.ShapeDtypeStruct((rows, width)...  136 us
    unnamed x3, local copies, waits for them, and re-layouts  4.7 us

profile of v6, /device:TPU:0, one launch (start us, length us, event | category | flops | bytes accessed | tf_op | source)
XLA Modules:
  0.0 142.5 jit_solution(7817481856945918098)
XLA Ops:
  1.3 1.4 copy.14
  2.7 1.4 copy.15
  4.1 136.4 %layer.1 = bf16[128,2048]{1,0:T(8,128)(2,1)} custom-call(s32[1,1]{1,0:T(1,128)S(6)} %copy.17.length_ref, s32[1,1]{1,0:T(1,128)S(6)} %copy.18.group_ref, s32[1,4]{1,0:T(1,128)} %owner_ref.1, bf16[128,2048]{1,0:T(8,128)(2,1)} %bitcast.17, bf16[2,128,2048]{2,1,0:T(8,128)(2,1)} %bitcast.16, bf16[2,384,2048]{2,1,0:T(8,128)(2,1)} %bitcast.14, ...), custom_call_target="tpu_custom_call" | custom-call | tf_op jit(solution)/shard_map/layer/pallas_call | solution.py:649
  140.6 1.9 %copy.19 = bf16[1,1,128,2048]{3,2,1,0:T(8,128)(2,1)} copy(bf16[1,1,128,2048]{3,2,1,0:T(8,128)(2,1)} %bitcast.15) | data formatting | bytes 1048576

commit v7 on v6

--- a/solution.py
+++ b/solution.py
@@ -297,7 +297,7 @@
         part[3, high, :] = part[3, high, :] + relay[g, 1]
         copies.start(("l_high", g), part.at[3, high], back.at[1, high], left)
 
-    tile = min(512, width)
+    tile = min(1024, width)
 
     def finish(g):
         for key in ("s1", "s2", "s3", "r_high", "l_low", "r_low", "l_high"):
@@ -434,7 +434,7 @@
     def run_experts(chunk):
         pairs = pairs_of[chunk]
         held = len(chunk) * CAP
-        tile = min(1024, width)
+        tile = width
         for start in range(0, width, tile):
             cols = pl.ds(start, tile)
             for n, (p, pair) in enumerate(pairs):

time: 143 us -> 143 us (level)
  no operation moved by 1% of the time
where the time goes in v7:
time: 143 us; the launch traced here: 142 us
  Pallas kernels  136 us (95%)
  local copies, waits for them, and re-layouts  4.7 us (3%)
    pallas_call x1, Pallas kernels, layer(): pl.pallas_call(layer_kernel, out_shape=jax.ShapeDtypeStruct((rows, width)...  136 us
    unnamed x3, local copies, waits for them, and re-layouts  4.7 us

profile of v7, /device:TPU:0, one launch (start us, length us, event | category | flops | bytes accessed | tf_op | source)
XLA Modules:
  0.0 141.8 jit_solution(8300272154924141671)
XLA Ops:
  1.3 1.4 copy.14
  2.7 1.4 copy.15
  4.1 135.8 %layer.1 = bf16[128,2048]{1,0:T(8,128)(2,1)} custom-call(s32[1,1]{1,0:T(1,128)S(6)} %copy.17.length_ref, s32[1,1]{1,0:T(1,128)S(6)} %copy.18.group_ref, s32[1,4]{1,0:T(1,128)} %owner_ref.1, bf16[128,2048]{1,0:T(8,128)(2,1)} %bitcast.17, bf16[2,128,2048]{2,1,0:T(8,128)(2,1)} %bitcast.16, bf16[2,384,2048]{2,1,0:T(8,128)(2,1)} %bitcast.14, ...), custom_call_target="tpu_custom_call" | custom-call | tf_op jit(solution)/shard_map/layer/pallas_call | solution.py:649
  139.9 1.9 %copy.19 = bf16[1,1,128,2048]{3,2,1,0:T(8,128)(2,1)} copy(bf16[1,1,128,2048]{3,2,1,0:T(8,128)(2,1)} %bitcast.15) | data formatting | bytes 1048576
